TPU v7x, 128 devices: a whole 4x4x4 slice. The times are simulated.
128 devices in a mesh: layer: 4 (over z), row: 32 (over y, x, core).
Axes of the slice: x: 4, y: 4, z: 4, core: 2. Of those that a mesh axis runs over, the one named last changes fastest.
Arguments:
- rhs_sub: float32 [4, 3, 4096, 256], P('layer', None, 'row'), may hold values from -6 to 6
- rhs_root: float32 [2048, 256], P('row'), may hold values from -6 to 6
- lower_inv: float32 [4, 3, 4096, 4096], P('layer', None, 'row'), may hold values from -0.09375 to 0.09375
- upper_inv: float32 [4, 3, 4096, 4096], P('layer', None, 'row'), may hold values from -0.09375 to 0.09375
- coupling_low: float32 [4, 3, 2048, 4096], P('layer', None, None, 'row'), may hold values from -0.0390625 to 0.0390625
- coupling_up: float32 [4, 3, 4096, 2048], P('layer', None, 'row'), may hold values from -0.1875 to 0.1875
- tile_mask: int32 [4, 3, 16, 32], P('layer', None, None, 'row'), may hold values 0 or 1
- root_inv: float32 [2048, 2048], P('row'), may hold values from -0.125 to 0.125
Outputs:
- sol_sub: float32 [4, 3, 4096, 256], P('layer', None, 'row')
- sol_root: float32 [2048, 256], P('row')
All inputs are finite; a program needn't handle non-finite values. No bound on the sum of `tile_mask` on one device may be relied on, other than what follows from the above.
Results may differ from a plain program's by a relative error of at most 0.0001.
Values sent between devices are 32-bit elements; how exact they have to be, the bound alone decides.
No kernel may reach another device: no remote copies, remote signals or barrier semaphores. Data moves between devices by JAX's collectives and lax.ppermute only.
A program may use at most 128 MiB of HBM per device.

v0:
```python
import functools

import jax
import jax.numpy as jnp
from jax import lax
from jax.experimental import pallas as pl
from jax.experimental.pallas import tpu as pltpu
from jax.sharding import PartitionSpec as P


K = 3
CH = 16
F32 = jnp.float32
BF16 = jnp.bfloat16


def row_id(y, x, c):
    return (y % 4) * 8 + (x % 4) * 2 + c % 2


def shift(array, da, db):
    pairs = []
    for y in range(4):
        for x in range(4):
            pairs.append((row_id(y, x, 0), row_id(y + db, x + da, 0)))
            pairs.append((row_id(y, x, 1), row_id(y + da, x + db, 1)))
    return lax.ppermute(array, "row", pairs)


def swap(array):
    return lax.ppermute(array, "row", [(i, i ^ 1) for i in range(32)])


SAME_CORE = [[2 * i + c for i in range(CH)] for c in range(2)]
SAME_CORE_ALL = [[l * 32 + 2 * i + c for l in range(4) for i in range(CH)] for c in range(2)]

FIRST = [(0, 0), (1, 0), (-1, 0), (2, 0), (0, -1), (0, 1), (1, -1), (1, 1)]
SECOND = [(-1, -1), (-1, 1), (2, -1), (2, 1)]
LATE = [(0, 2), (1, 2), (-1, 2), (2, 2)]


def gather_plane(own):
    move = lambda v, da, db: shift(v, da, db)
    right, left = move(own, -1, 0), move(own, 1, 0)
    far = move(own, 2, 0)
    ups, downs = [], []
    for value in (own, right, left, far):
        ups.append(move(value, 0, 1))
        downs.append(move(value, 0, -1))
    late = [move(downs[0], 0, -1), move(downs[1], 0, -1), move(ups[2], 0, 1), move(downs[3], 0, -1)]
    first = [own, right, left, far, ups[0], downs[0], ups[1], downs[1]]
    return first, [ups[2], downs[2], ups[3], downs[3]], late


def halves(value):
    top = value.astype(BF16)
    return top, (value - top.astype(F32)).astype(BF16)


def stacked(value, axis):
    return jnp.concatenate(halves(value), axis=axis)


def product(rows, w):
    n = rows.shape[0] // 2
    wide = jnp.dot(rows, w, preferred_element_type=F32)
    tall = wide[:n] + wide[n:]
    return tall[:, :128] + tall[:, 128:]


def chip_of(pos, da, db):
    core = pos[2]
    dy, dx = db + core * (da - db), da + core * (db - da)
    return lax.rem(pos[0] + dy + 4, 4) * 4 + lax.rem(pos[1] + dx + 4, 4)


def start_stage(pos, stage, pieces, own, part, lv, pv, sems):
    columns = [
        pl.ds(pl.multiple_of(chip_of(pos, da, db) * 256, 256), 256) for da, db in stage
    ]
    waits = []
    for k in range(K):
        copies = []
        for j, piece in enumerate(pieces):
            copies.append((piece.at[k], pv.at[k, j]))
        for j, column in enumerate(columns):
            here = slice(j * 256, j * 256 + 256)
            copies.append((own.at[k, :, column], lv.at[k, 0:128, here]))
            copies.append((part.at[k, :, column], lv.at[k, 128:256, here]))
        copies = [
            pltpu.make_async_copy(src, dst, sems.at[k, i]) for i, (src, dst) in enumerate(copies)
        ]
        for copy in copies:
            copy.start()
        waits.append(copies)
    return waits


def stage_product(waits, k, lv, pv, w):
    for copy in waits[k]:
        copy.wait()
    for j in range(pv.shape[1]):
        w[k, j * 256 : j * 256 + 256, :] = stacked(pv[k, j], 1)
    return product(stacked(lv[k], 0), w[k])


def add_kernel(stage, has_total, pos, *refs):
    total, refs = (refs[0], refs[1:]) if has_total else (None, refs)
    pieces = refs[: len(stage)]
    own, part, out, lv, pv, w, sems = refs[len(stage) :]
    waits = start_stage(pos, stage, pieces, own, part, lv, pv, sems)
    for k in range(K):
        value = stage_product(waits, k, lv, pv, w)
        out[k] = total[k] + value if has_total else value


def lower_kernel(n, pos, mask_own, mask_part, total, *refs):
    pieces = refs[:n]
    own, part, low_own, low_part, interim, out, lv, pv, w, lo_v, lp_v, sems, low_sems = refs[n:]
    waits = start_stage(pos, LATE, pieces, own, part, lv, pv, sems)
    low_copies = []
    for c in range(4):
        rows = slice(c * 512, c * 512 + 512)
        low_copies.append(
            [
                pltpu.make_async_copy(low_own.at[:, rows], lo_v.at[:, rows], low_sems.at[c, 0]),
                pltpu.make_async_copy(low_part.at[:, rows], lp_v.at[:, rows], low_sems.at[c, 1]),
            ]
        )
        for copy in low_copies[-1]:
            copy.start()
    weights = []
    for k in range(K):
        value = total[k] + stage_product(waits, k, lv, pv, w)
        interim[k] = value
        weights.append(stacked(value, 1))
    for c in range(4):
        for copy in low_copies[c]:
            copy.wait()
        roots = None
        for k in range(K):
            tiles = []
            for i in range(4 * c, 4 * c + 4):
                rows = slice(i * 128, i * 128 + 128)
                tiles.append(
                    jnp.concatenate(
                        [
                            lo_v[k, rows, :] * mask_own[k, i, 0].astype(F32),
                            lp_v[k, rows, :] * mask_part[k, i, 0].astype(F32),
                        ],
                        axis=1,
                    )
                )
            value = product(stacked(jnp.concatenate(tiles, axis=0), 0), weights[k])
            roots = value if roots is None else roots + value
        for i in range(4):
            flat = roots[i * 128 : i * 128 + 128].T
            for z in range(4):
                out[z, 4 * c + i] = flat[z * 32 : z * 32 + 32]


def upper_kernel(n, pos, total, *refs):
    pieces = refs[:n]
    own, part, out, out_part, lv, pv, w, sems = refs[n:]
    waits = start_stage(pos, LATE, pieces, own, part, lv, pv, sems)
    lanes = pl.ds(pl.multiple_of(pos[2] * 128, 128), 128)
    for k in range(K):
        value = total[k] + stage_product(waits, k, lv, pv, w)
        out[k, :, lanes] = value[:128]
        out_part[k] = value[128:]


def couple_kernel(pos, root, interim, up, residue, up_v, w, sems):
    copies = [pltpu.make_async_copy(up.at[k], up_v.at[k], sems.at[k]) for k in range(K)]
    for copy in copies:
        copy.start()
    for i in range(CH):
        flat = jnp.concatenate([root[z, i] for z in range(4)], axis=0)
        w[i * 128 : i * 128 + 128, :] = stacked(flat.T, 1)
    here = pl.ds(pl.multiple_of(pos[2] * 128, 128), 128)
    there = pl.ds(pl.multiple_of((1 - pos[2]) * 128, 128), 128)
    for k in range(K):
        copies[k].wait()
        value = interim[k] - product(up_v[k], w[...])
        residue[k, here, :] = value[:128]
        residue[k, there, :] = value[128:]


def up_kernel(mask_own, mask_part, own, part, out):
    k = pl.program_id(0)
    for n, (mask, ref) in enumerate(((mask_own, own), (mask_part, part))):
        for i in range(CH):
            lanes = slice(i * 128, i * 128 + 128)
            top, low = halves(ref[0, :, lanes] * mask[k, i, 0].astype(F32))
            out[0, n * 128 : n * 128 + 128, lanes] = top
            out[0, 256 + n * 128 : 384 + n * 128, lanes] = low


BIG = 58
VMEM = pl.BlockSpec(memory_space=pltpu.VMEM)
HBM = pl.BlockSpec(memory_space=pltpu.HBM)
SMEM = pl.BlockSpec(memory_space=pltpu.SMEM)


def sds(*shape, dtype=F32):
    return jax.ShapeDtypeStruct(shape, dtype)


def limit(mib):
    return pltpu.CompilerParams(vmem_limit_bytes=mib * 1024 * 1024)


def stage_scratch(stage, pieces):
    n = len(stage)
    return [
        pltpu.VMEM((K, 256, n * 256), F32),
        pltpu.VMEM((K, n, 256, 128), F32),
        pltpu.VMEM((K, n * 256, 256), BF16),
        pltpu.SemaphoreType.DMA((K, 2 * n + len(pieces))),
    ]


def run_add(pos, stage, total, pieces, own, part):
    totals = [] if total is None else [total]
    return pl.pallas_call(
        functools.partial(add_kernel, stage, total is not None),
        out_shape=sds(K, 256, 128),
        in_specs=[SMEM] + [VMEM] * len(totals) + [HBM] * (len(pieces) + 2),
        out_specs=VMEM,
        scratch_shapes=stage_scratch(stage, pieces),
        compiler_params=limit(BIG),
    )(pos, *totals, *pieces, own, part)


def run_lower(pos, mask_own, mask_part, total, pieces, own, part, low_own, low_part):
    scratch = stage_scratch(LATE, pieces)
    return pl.pallas_call(
        functools.partial(lower_kernel, len(pieces)),
        out_shape=(sds(K, 256, 128), sds(4, CH, 32, 128)),
        in_specs=[SMEM] * 3 + [VMEM] + [HBM] * (len(pieces) + 4),
        out_specs=(VMEM, VMEM),
        scratch_shapes=scratch[:3]
        + [
            pltpu.VMEM((K, 2048, 128), F32),
            pltpu.VMEM((K, 2048, 128), F32),
            scratch[3],
            pltpu.SemaphoreType.DMA((4, 2)),
        ],
        compiler_params=limit(BIG),
    )(pos, mask_own, mask_part, total, *pieces, own, part, low_own, low_part)


def run_upper(pos, total, pieces, own, part):
    return pl.pallas_call(
        functools.partial(upper_kernel, len(pieces)),
        out_shape=(sds(K, 128, 256), sds(K, 128, 128)),
        in_specs=[SMEM, VMEM] + [HBM] * (len(pieces) + 2),
        out_specs=(VMEM, VMEM),
        scratch_shapes=stage_scratch(LATE, pieces),
        compiler_params=limit(BIG),
    )(pos, total, *pieces, own, part)


def run_couple(pos, root, interim, up):
    return pl.pallas_call(
        couple_kernel,
        out_shape=sds(K, 256, 128),
        in_specs=[SMEM, VMEM, VMEM, HBM],
        out_specs=VMEM,
        scratch_shapes=[
            pltpu.VMEM((K, 512, 2048), BF16),
            pltpu.VMEM((2048, 256), BF16),
            pltpu.SemaphoreType.DMA((K,)),
        ],
        compiler_params=limit(BIG),
    )(pos, root, interim, up)


def run_up(mask_own, mask_part, own, part):
    block = pl.BlockSpec((1, 128, 2048), lambda k: (k, 0, 0))
    return pl.pallas_call(
        up_kernel,
        out_shape=pltpu.HBM((K, 512, 2048), BF16),
        grid=(K,),
        in_specs=[SMEM, SMEM, block, block],
        out_specs=pl.BlockSpec((1, 512, 2048), lambda k: (k, 0, 0)),
        compiler_params=limit(BIG),
    )(mask_own, mask_part, own, part)


def body(rhs_sub, rhs_root, lower_inv, upper_inv, coupling_low, coupling_up, tile_mask, root_inv):
    me = lax.axis_index("row")
    layer = lax.axis_index("layer")
    core = me % 2
    pos = jnp.stack([me // 8, me // 2 % 4, core]).astype(jnp.int32)
    first = core == 0

    def to_columns(a):
        left, right = a[..., :128], a[..., 128:]
        mine, other = jnp.where(first, left, right), jnp.where(first, right, left)
        got = swap(other)
        return jnp.where(
            first, jnp.concatenate([mine, got], axis=-2), jnp.concatenate([got, mine], axis=-2)
        )

    block = to_columns(rhs_sub[0])
    block, rhs_root, lower_own, low_own, up_own, root_inv, tile_mask = lax.optimization_barrier(
        (block, rhs_root, lower_inv[0], coupling_low[0], coupling_up[0], root_inv, tile_mask)
    )
    first_part, second_part, late = gather_plane(block)
    lower_part = swap(lower_own)
    mask_own = tile_mask[0]
    mask_part = swap(mask_own)
    right = lax.dynamic_slice_in_dim(to_columns(rhs_root).T, layer * 32, 32, 0)
    low_part = swap(low_own)
    up_part = swap(up_own)
    up = run_up(mask_own, mask_part, up_own, up_part)

    total = run_add(pos, FIRST, None, first_part, lower_own, lower_part)
    total = run_add(pos, SECOND, total, second_part, lower_own, lower_part)
    upper_own, root_inv = lax.optimization_barrier((upper_inv[0], root_inv, first_part[1]))[:2]
    upper_part = swap(upper_own)
    root_other = swap(root_inv)
    root_rows = jnp.where(
        first,
        jnp.concatenate([root_inv, root_other], axis=0),
        jnp.concatenate([root_other, root_inv], axis=0),
    )
    interim, parts = run_lower(
        pos, mask_own, mask_part, total, late, lower_own, lower_part, low_own, low_part
    )
    moved = lax.all_to_all(
        parts.reshape(64, 32, 128), ("layer", "row"), 0, 0, tiled=True,
        axis_index_groups=SAME_CORE_ALL,
    )
    reduced = right - jnp.sum(moved, axis=0)
    everywhere = lax.all_to_all(
        jnp.broadcast_to(reduced[None], (CH, 32, 128)), "row", 0, 0, tiled=True,
        axis_index_groups=SAME_CORE,
    )
    solved = jnp.einsum(
        "icr,oir->co", everywhere, root_rows.reshape(128, CH, 128), precision=lax.Precision.HIGHEST
    )
    root = lax.all_to_all(
        jnp.broadcast_to(solved[None], (64, 32, 128)), ("layer", "row"), 0, 0, tiled=True,
        axis_index_groups=SAME_CORE_ALL,
    ).reshape(4, CH, 32, 128)
    residue = run_couple(pos, root, interim, up)
    first_part, second_part, late = gather_plane(residue)
    total = run_add(pos, FIRST, None, first_part, upper_own, upper_part)
    total = run_add(pos, SECOND, total, second_part, upper_own, upper_part)
    out, out_part = run_upper(pos, total, late, upper_own, upper_part)
    sol_sub = lax.dynamic_update_slice(out, swap(out_part), (0, 0, (1 - core) * 128))

    chip = me // 2
    mine = lax.dynamic_index_in_dim(root, chip, 1, keepdims=False).reshape(128, 128).T
    own_rows = lax.dynamic_slice_in_dim(mine, core * 64, 64, 0)
    other_rows = swap(lax.dynamic_slice_in_dim(mine, (1 - core) * 64, 64, 0))
    sol_root = jnp.where(
        first,
        jnp.concatenate([own_rows, other_rows], axis=-1),
        jnp.concatenate([other_rows, own_rows], axis=-1),
    )
    return sol_sub[None], sol_root


def solution(mesh):
    return jax.shard_map(
        body,
        mesh=mesh,
        in_specs=(
            P("layer", None, "row", None),
            P("row", None),
            P("layer", None, "row", None),
            P("layer", None, "row", None),
            P("layer", None, None, "row"),
            P("layer", None, "row", None),
            P("layer", None, None, "row"),
            P("row", None),
        ),
        out_specs=(P("layer", None, "row", None), P("row", None)),
        check_vma=False,
    )
```

profile of v0, /device:TPU:1, one launch (start us, length us, event | category | flops | bytes accessed | tf_op | source)
XLA Modules:
  0.0 242.8 jit_solution(3854019897857226694)
XLA Ops:
  0.6 1.1 slice_select_fusion.1
  1.7 1.5 collective-permute-start
  3.2 1.1 collective-permute-done
  4.7 2.8 %collective-permute-start.3 = (f32[3,256,128]{2,1,0:T(8,128)S(1)}, f32[3,256,128]{2,1,0:T(8,128)S(1)}, u32[]{:S(2)}, u32[]{:S(2)}) collective-permute-start(f32[3,256,128]{2,1,0:T(8,128)S(1)} %maximum_select_fusion.2.refs_0_), channel_id=1, source_target_pairs={{0,6},{1,25},{2,0},{3,27},{4,2},{5,29},{6,4},{7,31},{8,14},{9,1},{... | collective-permute-start | bytes 1179656 | tf_op jit(solution)/shard_map/ppermute | solution.py:27
  7.6 4.7 %collective-permute-done.3.refs_1_ = f32[3,256,128]{2,1,0:T(8,128)S(1)} collective-permute-done((f32[3,256,128]{2,1,0:T(8,128)S(1)}, f32[3,256,128]{2,1,0:T(8,128)S(1)}, u32[]{:S(2)}, u32[]{:S(2)}) %collective-permute-start.3) | collective-permute-done | bytes 393248 | tf_op jit(solution)/shard_map/ppermute | solution.py:27
  12.3 0.7 collective-permute-start.29
  13.1 0.7 collective-permute-start.19
  13.8 1.3 collective-permute-start.4
  15.1 1.4 copy.30.mask_own
  16.5 11.9 %collective-permute-done.2.mask_part = s32[3,16,1]{2,1,0:T(8,128)} collective-permute-done((s32[3,16,1]{2,1,0:T(8,128)}, s32[3,16,1]{2,1,0:T(8,128)}, u32[]{:S(2)}, u32[]{:S(2)}) %collective-permute-start.2) | collective-permute-done | bytes 224 | tf_op jit(solution)/shard_map/ppermute | solution.py:31
  28.4 3.0 %collective-permute-start.5 = (f32[3,256,128]{2,1,0:T(8,128)S(1)}, f32[3,256,128]{2,1,0:T(8,128)S(1)}, u32[]{:S(2)}, u32[]{:S(2)}) collective-permute-start(f32[3,256,128]{2,1,0:T(8,128)S(1)} %maximum_select_fusion.2.refs_0_), channel_id=1, source_target_pairs={{0,4},{1,17},{2,6},{3,19},{4,0},{5,21},{6,2},{7,23},{8,12},{9,25},... | collective-permute-start | bytes 1179656 | tf_op jit(solution)/shard_map/ppermute | solution.py:27
  31.4 1.2 collective-permute-start.6
  32.6 5.5 %collective-permute-done.5.refs_3_ = f32[3,256,128]{2,1,0:T(8,128)S(1)} collective-permute-done((f32[3,256,128]{2,1,0:T(8,128)S(1)}, f32[3,256,128]{2,1,0:T(8,128)S(1)}, u32[]{:S(2)}, u32[]{:S(2)}) %collective-permute-start.5) | collective-permute-done | bytes 393248 | tf_op jit(solution)/shard_map/ppermute | solution.py:27
  38.1 4.4 %collective-permute-start.7 = (f32[3,256,128]{2,1,0:T(8,128)S(1)}, f32[3,256,128]{2,1,0:T(8,128)S(1)}, u32[]{:S(2)}, u32[]{:S(2)}) collective-permute-start(f32[3,256,128]{2,1,0:T(8,128)S(1)} %maximum_select_fusion.2.refs_0_), channel_id=1, source_target_pairs={{0,24},{1,7},{2,26},{3,1},{4,28},{5,3},{6,30},{7,5},{8,0},{9,15},{... | collective-permute-start | bytes 1179656 | tf_op jit(solution)/shard_map/ppermute | solution.py:27
  42.5 0.7 collective-permute-start.8
  43.2 4.0 %collective-permute-done.7.refs_5_ = f32[3,256,128]{2,1,0:T(8,128)S(1)} collective-permute-done((f32[3,256,128]{2,1,0:T(8,128)S(1)}, f32[3,256,128]{2,1,0:T(8,128)S(1)}, u32[]{:S(2)}, u32[]{:S(2)}) %collective-permute-start.7) | collective-permute-done | bytes 393248 | tf_op jit(solution)/shard_map/ppermute | solution.py:27
  47.2 3.4 %collective-permute-start.9 = (f32[3,256,128]{2,1,0:T(8,128)}, f32[3,256,128]{2,1,0:T(8,128)S(1)}, u32[]{:S(2)}, u32[]{:S(2)}) collective-permute-start(f32[3,256,128]{2,1,0:T(8,128)} %copy-done.3), channel_id=1, source_target_pairs={{0,24},{1,7},{2,26},{3,1},{4,28},{5,3},{6,30},{7,5},{8,0},{9,15},{... | collective-permute-start | bytes 1179656 | tf_op jit(solution)/shard_map/ppermute | solution.py:27
  50.8 4.8 %collective-permute-done.9.refs_7_ = f32[3,256,128]{2,1,0:T(8,128)S(1)} collective-permute-done((f32[3,256,128]{2,1,0:T(8,128)}, f32[3,256,128]{2,1,0:T(8,128)S(1)}, u32[]{:S(2)}, u32[]{:S(2)}) %collective-permute-start.9) | collective-permute-done | bytes 393248 | tf_op jit(solution)/shard_map/ppermute | solution.py:27
  55.6 3.4 %collective-permute-start.12 = (f32[3,256,128]{2,1,0:T(8,128)}, f32[3,256,128]{2,1,0:T(8,128)S(1)}, u32[]{:S(2)}, u32[]{:S(2)}) collective-permute-start(f32[3,256,128]{2,1,0:T(8,128)} %collective-permute-done.4.refs_2_), channel_id=1, source_target_pairs={{0,24},{1,7},{2,26},{3,1},{4,28},{5,3},{6,30},{7,5},{8,0},{9,15},{... | collective-permute-start | bytes 1179656 | tf_op jit(solution)/shard_map/ppermute | solution.py:27
  59.3 4.8 %collective-permute-done.12.refs_2_ = f32[3,256,128]{2,1,0:T(8,128)S(1)} collective-permute-done((f32[3,256,128]{2,1,0:T(8,128)}, f32[3,256,128]{2,1,0:T(8,128)S(1)}, u32[]{:S(2)}, u32[]{:S(2)}) %collective-permute-start.12) | collective-permute-done | bytes 393248 | tf_op jit(solution)/shard_map/ppermute | solution.py:27
  64.1 3.4 %collective-permute-start.14 = (f32[3,256,128]{2,1,0:T(8,128)S(1)}, f32[3,256,128]{2,1,0:T(8,128)}, u32[]{:S(2)}, u32[]{:S(2)}) collective-permute-start(f32[3,256,128]{2,1,0:T(8,128)S(1)} %collective-permute-done.5.refs_3_), channel_id=1, source_target_pairs={{0,24},{1,7},{2,26},{3,1},{4,28},{5,3},{6,30},{7,5},{8,0},{9,15},{... | collective-permute-start | bytes 1179656 | tf_op jit(solution)/shard_map/ppermute | solution.py:27
  67.6 4.6 %collective-permute-done.14.refs_4_ = f32[3,256,128]{2,1,0:T(8,128)} collective-permute-done((f32[3,256,128]{2,1,0:T(8,128)S(1)}, f32[3,256,128]{2,1,0:T(8,128)}, u32[]{:S(2)}, u32[]{:S(2)}) %collective-permute-start.14) | collective-permute-done | bytes 393248 | tf_op jit(solution)/shard_map/ppermute | solution.py:27
  72.2 3.2 %collective-permute-start.16 = (f32[3,256,128]{2,1,0:T(8,128)S(1)}, f32[3,256,128]{2,1,0:T(8,128)S(1)}, u32[]{:S(2)}, u32[]{:S(2)}) collective-permute-start(f32[3,256,128]{2,1,0:T(8,128)S(1)} %collective-permute-done.9.refs_7_), channel_id=1, source_target_pairs={{0,24},{1,7},{2,26},{3,1},{4,28},{5,3},{6,30},{7,5},{8,0},{9,15},{... | collective-permute-start | bytes 1179656 | tf_op jit(solution)/shard_map/ppermute | solution.py:27
  75.5 1.0 collective-permute-done.15.refs_0_
  76.5 4.9 %collective-permute-start.21 = (f32[3,128,2048]{2,1,0:T(8,128)}, f32[3,128,2048]{2,1,0:T(8,128)}, u32[]{:S(2)}, u32[]{:S(2)}) collective-permute-start(f32[3,128,2048]{2,1,0:T(8,128)} %bitcast.48), channel_id=1, source_target_pairs={{0,1},{1,0},{2,3},{3,2},{4,5},{5,4},{6,7},{7,6},{8,9},{9,8},{10,11... | collective-permute-start | bytes 9437192 | tf_op jit(solution)/shard_map/ppermute | solution.py:31
  82.1 2.4 collective-permute-start.18
  85.2 7.5 %shard_map.95.refs_0_ = f32[3,256,128]{2,1,0:T(8,128)} custom-call(s32[3]{0:T(128)} %pad_add_fusion.pos, f32[3,256,128]{2,1,0:T(8,128)} %copy-done.2, f32[3,256,128]{2,1,0:T(8,128)} %copy-done.3, f32[3,256,128]{2,1,0:T(8,128)} %collective-permute-done.4.refs_2_, f32[3,256,128]{2,1,0:T(8,128)} %copy-done.4, f32[3,256,128]{2,1,0:T(8,128)} %copy-done.5, ...), custom_call_target="tpu_custom_call" | custom-call | tf_op jit(solution)/shard_map/pallas_call | solution.py:225
  92.7 5.4 %shard_map.96.total = f32[3,256,128]{2,1,0:T(8,128)} custom-call(s32[3]{0:T(128)} %pad_add_fusion.pos, f32[3,256,128]{2,1,0:T(8,128)} %shard_map.95.refs_0_, f32[3,256,128]{2,1,0:T(8,128)} %collective-permute-done.11.refs_1_, f32[3,256,128]{2,1,0:T(8,128)} %copy-done.9, f32[3,256,128]{2,1,0:T(8,128)} %collective-permute-done.13.refs_3_, ...), custom_call_target="tpu_custom_call" | custom-call | tf_op jit(solution)/shard_map/pallas_call | solution.py:225
  98.2 1.6 copy-done.1
  99.8 10.7 %shard_map.97 = (f32[3,256,128]{2,1,0:T(8,128)}, f32[4,16,32,128]{3,2,1,0:T(8,128)}) custom-call(s32[3]{0:T(128)} %pad_add_fusion.pos, s32[3,16,1]{2,1,0:T(8,128)} %copy.30.mask_own, s32[3,16,1]{2,1,0:T(8,128)} %collective-permute-done.2.mask_part, f32[3,256,128]{2,1,0:T(8,128)} %shard_map.96.total, f32[3,256,128]{2,1,0:T(8,128)} %copy-done.10, ...), custom_call_target="tpu_custom_call" | custom-call | tf_op jit(solution)/shard_map/pallas_call | solution.py:237
  110.5 9.8 %all-to-all-start = ((f32[64,32,128]{2,1,0:T(8,128)}), f32[64,32,128]{2,1,0:T(8,128)S(1)}, u32[]{:S(2)}, u32[]{:S(2)}) async-start(f32[64,32,128]{2,1,0:T(8,128)} %bitcast.50), calls=%async_computation | async-start | bytes 2097152 | tf_op jit(solution)/shard_map/all_to_all | solution.py:332
  120.4 5.7 %collective-permute-start.20 = (f32[64,2048]{1,0:T(8,128)}, f32[64,2048]{1,0:T(8,128)S(1)}, u32[]{:S(2)}, u32[]{:S(2)}) collective-permute-start(f32[64,2048]{1,0:T(8,128)} %param.15), channel_id=1, source_target_pairs={{0,1},{1,0},{2,3},{3,2},{4,5},{5,4},{6,7},{7,6},{8,9},{9,8},{10,11... | collective-permute-start | bytes 1572872 | tf_op jit(solution)/shard_map/ppermute | solution.py:31
  126.3 1.1 copy_bitcast_fusion.1
  127.4 6.8 %all-to-all-done = f32[64,32,128]{2,1,0:T(8,128)S(1)} async-done(((f32[64,32,128]{2,1,0:T(8,128)}), f32[64,32,128]{2,1,0:T(8,128)S(1)}, u32[]{:S(2)}, u32[]{:S(2)}) %all-to-all-start) | async-done | bytes 1048608 | tf_op jit(solution)/shard_map/all_to_all | solution.py:332
  134.4 0.7 broadcast_in_dim.8
  135.1 3.5 %all-to-all-start.1 = ((f32[16,32,128]{2,1,0:T(8,128)}), f32[16,32,128]{2,1,0:T(8,128)S(1)}, u32[]{:S(2)}, u32[]{:S(2)}) async-start(f32[16,32,128]{2,1,0:T(8,128)} %broadcast_in_dim.8), calls=%async_computation.1 | async-start | bytes 524288 | tf_op jit(solution)/shard_map/all_to_all | solution.py:337
  138.7 7.4 %all-to-all-done.1 = f32[16,32,128]{2,1,0:T(8,128)S(1)} async-done(((f32[16,32,128]{2,1,0:T(8,128)}), f32[16,32,128]{2,1,0:T(8,128)S(1)}, u32[]{:S(2)}, u32[]{:S(2)}) %all-to-all-start.1) | async-done | bytes 262176 | tf_op jit(solution)/shard_map/all_to_all | solution.py:337
  146.2 1.1 convolution_bitcast_fusion
  147.3 1.1 broadcast_in_dim.18
  148.4 4.9 %all-to-all-start.2 = ((f32[64,32,128]{2,1,0:T(8,128)}), f32[64,32,128]{2,1,0:T(8,128)S(1)}, u32[]{:S(2)}, u32[]{:S(2)}) async-start(f32[64,32,128]{2,1,0:T(8,128)} %broadcast_in_dim.18), calls=%async_computation.2 | async-start | bytes 2097152 | tf_op jit(solution)/shard_map/all_to_all | solution.py:344
  153.3 7.3 %shard_map.98.up = bf16[3,512,2048]{2,1,0:T(8,128)(2,1)} custom-call(s32[3,16,1]{2,1,0:T(8,128)} %copy.30.mask_own, s32[3,16,1]{2,1,0:T(8,128)} %collective-permute-done.2.mask_part, f32[3,128,2048]{2,1,0:T(8,128)} %bitcast.49, f32[3,128,2048]{2,1,0:T(8,128)} %collective-permute-done.21.part), custom_call_target="tpu_custom_call" | custom-call | tf_op jit(solution)/shard_map/pallas_call | solution.py:281
  160.6 6.2 %all-to-all-done.2 = f32[64,32,128]{2,1,0:T(8,128)S(1)} async-done(((f32[64,32,128]{2,1,0:T(8,128)}), f32[64,32,128]{2,1,0:T(8,128)S(1)}, u32[]{:S(2)}, u32[]{:S(2)}) %all-to-all-start.2) | async-done | bytes 1048608 | tf_op jit(solution)/shard_map/all_to_all | solution.py:344
  166.9 1.0 copy-done
  167.9 6.8 %shard_map.99.refs_0_ = f32[3,256,128]{2,1,0:T(8,128)} custom-call(s32[3]{0:T(128)} %pad_add_fusion.pos, f32[4,16,32,128]{3,2,1,0:T(8,128)} %bitcast.44, f32[3,256,128]{2,1,0:T(8,128)} %get-tuple-element.23.interim, bf16[3,512,2048]{2,1,0:T(8,128)(2,1)} %shard_map.98.up), custom_call_target="tpu_custom_call" | custom-call | tf_op jit(solution)/shard_map/pallas_call | solution.py:265
  174.9 1.4 collective-permute-start.23
  177.2 2.4 collective-permute-start.26
  179.6 2.0 collective-permute-done.22.refs_1_
  181.9 5.3 %collective-permute-done.23.refs_2_ = f32[3,256,128]{2,1,0:T(8,128)S(1)} collective-permute-done((f32[3,256,128]{2,1,0:T(8,128)}, f32[3,256,128]{2,1,0:T(8,128)S(1)}, u32[]{:S(2)}, u32[]{:S(2)}) %collective-permute-start.23) | collective-permute-done | bytes 393248 | tf_op jit(solution)/shard_map/ppermute | solution.py:27
  187.1 0.8 collective-permute-start.28
  188.6 2.0 collective-permute-start.31
  190.7 1.4 collective-permute-start.32
  192.1 6.2 %collective-permute-done.28.refs_7_ = f32[3,256,128]{2,1,0:T(8,128)S(1)} collective-permute-done((f32[3,256,128]{2,1,0:T(8,128)S(1)}, f32[3,256,128]{2,1,0:T(8,128)S(1)}, u32[]{:S(2)}, u32[]{:S(2)}) %collective-permute-start.28) | collective-permute-done | bytes 393248 | tf_op jit(solution)/shard_map/ppermute | solution.py:27
  198.3 1.3 collective-permute-start.34
  199.6 1.6 collective-permute-done.30.refs_1_
  201.1 2.6 %collective-permute-done.31.refs_2_ = f32[3,256,128]{2,1,0:T(8,128)S(1)} collective-permute-done((f32[3,256,128]{2,1,0:T(8,128)S(1)}, f32[3,256,128]{2,1,0:T(8,128)S(1)}, u32[]{:S(2)}, u32[]{:S(2)}) %collective-permute-start.31) | collective-permute-done | bytes 393248 | tf_op jit(solution)/shard_map/ppermute | solution.py:27
  204.0 3.6 %collective-permute-done.33.refs_4_ = f32[3,256,128]{2,1,0:T(8,128)S(1)} collective-permute-done((f32[3,256,128]{2,1,0:T(8,128)S(1)}, f32[3,256,128]{2,1,0:T(8,128)S(1)}, u32[]{:S(2)}, u32[]{:S(2)}) %collective-permute-start.33) | collective-permute-done | bytes 393248 | tf_op jit(solution)/shard_map/ppermute | solution.py:27
  207.6 2.1 collective-permute-start.37
  209.8 0.8 constant_dynamic-slice_fusion
  210.7 7.5 %shard_map.100.refs_0_ = f32[3,256,128]{2,1,0:T(8,128)} custom-call(s32[3]{0:T(128)} %pad_add_fusion.pos, f32[3,256,128]{2,1,0:T(8,128)} %shard_map.99.refs_0_, f32[3,256,128]{2,1,0:T(8,128)} %copy-done.11, f32[3,256,128]{2,1,0:T(8,128)} %copy-done.13, f32[3,256,128]{2,1,0:T(8,128)} %copy-done.14, f32[3,256,128]{2,1,0:T(8,128)} %copy-done.16, ...), custom_call_target="tpu_custom_call" | custom-call | tf_op jit(solution)/shard_map/pallas_call | solution.py:225
  218.2 5.4 %shard_map.101.total = f32[3,256,128]{2,1,0:T(8,128)} custom-call(s32[3]{0:T(128)} %pad_add_fusion.pos, f32[3,256,128]{2,1,0:T(8,128)} %shard_map.100.refs_0_, f32[3,256,128]{2,1,0:T(8,128)} %copy-done.18, f32[3,256,128]{2,1,0:T(8,128)} %copy-done.21, f32[3,256,128]{2,1,0:T(8,128)} %collective-permute-done.32.refs_3_, f32[3,256,128]{2,1,0:T(8,128)} %copy-done.20, ...), custom_call_target="tpu_custom_call" | custom-call | tf_op jit(solution)/shard_map/pallas_call | solution.py:225
  223.7 5.5 %shard_map.102 = (f32[3,128,256]{2,1,0:T(8,128)}, f32[3,128,128]{2,1,0:T(8,128)}) custom-call(s32[3]{0:T(128)} %pad_add_fusion.pos, f32[3,256,128]{2,1,0:T(8,128)} %shard_map.101.total, f32[3,256,128]{2,1,0:T(8,128)} %collective-permute-done.34.refs_0_, f32[3,256,128]{2,1,0:T(8,128)} %collective-permute-done.35.refs_1_, ...), custom_call_target="tpu_custom_call" | custom-call | tf_op jit(solution)/shard_map/pallas_call | solution.py:254
  229.1 10.8 %collective-permute-start.38 = (f32[3,128,128]{2,1,0:T(8,128)}, f32[3,128,128]{2,1,0:T(8,128)S(1)}, u32[]{:S(2)}, u32[]{:S(2)}) collective-permute-start(f32[3,128,128]{2,1,0:T(8,128)} %get-tuple-element.27), channel_id=1, source_target_pairs={{0,1},{1,0},{2,3},{3,2},{4,5},{5,4},{6,7},{7,6},{8,9},{9,8},{10,11... | collective-permute-start | bytes 589832 | tf_op jit(solution)/shard_map/ppermute | solution.py:31
  240.2 1.2 collective-permute-done.39
  241.4 0.7 copy.36
  (94 shorter events, 6.3 us)
Async XLA Ops:
  1.7 2.5 %collective-permute-start = (f32[3,128,128]{2,1,0:T(8,128)S(1)}, f32[3,128,128]{2,1,0:T(8,128)S(1)}, u32[]{:S(2)}, u32[]{:S(2)}) collective-permute-start(f32[3,128,128]{2,1,0:T(8,128)S(1)} %get-tuple-element.33), channel_id=1, source_target_pairs={{0,1},{1,0},{2,3},{3,2},{4,5},{5,4},{6,7},{7,6},{8,9},{9,8},{10,11... | collective-permute-start | bytes 589832 | tf_op jit(solution)/shard_map/ppermute | solution.py:31
  4.3 80.9 %copy-start.2 = (f32[3,256,128]{2,1,0:T(8,128)}, f32[3,256,128]{2,1,0:T(8,128)S(1)}, u32[]{:S(2)}) copy-start(f32[3,256,128]{2,1,0:T(8,128)S(1)} %maximum_select_fusion.2.refs_0_) | copy-start | bytes 1179652
  4.3 77.2 %collective-permute-start.10 = (f32[3,128,4096]{2,1,0:T(8,128)}, f32[3,128,4096]{2,1,0:T(8,128)}, u32[]{:S(2)}, u32[]{:S(2)}) collective-permute-start(f32[3,128,4096]{2,1,0:T(8,128)} %bitcast.36), channel_id=1, source_target_pairs={{0,1},{1,0},{2,3},{3,2},{4,5},{5,4},{6,7},{7,6},{8,9},{9,8},{10,11... | collective-permute-start | bytes 18874376 | tf_op jit(solution)/shard_map/ppermute | solution.py:31
  4.7 7.6 %collective-permute-start.3 = (f32[3,256,128]{2,1,0:T(8,128)S(1)}, f32[3,256,128]{2,1,0:T(8,128)S(1)}, u32[]{:S(2)}, u32[]{:S(2)}) collective-permute-start(f32[3,256,128]{2,1,0:T(8,128)S(1)} %maximum_select_fusion.2.refs_0_), channel_id=1, source_target_pairs={{0,6},{1,25},{2,0},{3,27},{4,2},{5,29},{6,4},{7,31},{8,14},{9,1},{... | collective-permute-start | bytes 1179656 | tf_op jit(solution)/shard_map/ppermute | solution.py:27
  12.3 164.9 %collective-permute-start.29 = (f32[3,128,4096]{2,1,0:T(8,128)}, f32[3,128,4096]{2,1,0:T(8,128)}, u32[]{:S(2)}, u32[]{:S(2)}) collective-permute-start(f32[3,128,4096]{2,1,0:T(8,128)} %bitcast.40), channel_id=1, source_target_pairs={{0,1},{1,0},{2,3},{3,2},{4,5},{5,4},{6,7},{7,6},{8,9},{9,8},{10,11... | collective-permute-start | bytes 18874376 | tf_op jit(solution)/shard_map/ppermute | solution.py:31
  13.1 85.1 %collective-permute-start.19 = (f32[3,2048,128]{2,1,0:T(8,128)}, f32[3,2048,128]{2,1,0:T(8,128)S(1)}, u32[]{:S(2)}, u32[]{:S(2)}) collective-permute-start(f32[3,2048,128]{2,1,0:T(8,128)} %bitcast.46), channel_id=1, source_target_pairs={{0,1},{1,0},{2,3},{3,2},{4,5},{5,4},{6,7},{7,6},{8,9},{9,8},{10,11... | collective-permute-start | bytes 9437192 | tf_op jit(solution)/shard_map/ppermute | solution.py:31
  13.8 17.6 %collective-permute-start.4 = (f32[3,256,128]{2,1,0:T(8,128)S(1)}, f32[3,256,128]{2,1,0:T(8,128)}, u32[]{:S(2)}, u32[]{:S(2)}) collective-permute-start(f32[3,256,128]{2,1,0:T(8,128)S(1)} %maximum_select_fusion.2.refs_0_), channel_id=1, source_target_pairs={{0,2},{1,9},{2,4},{3,11},{4,6},{5,13},{6,0},{7,15},{8,10},{9,17},{... | collective-permute-start | bytes 1179656 | tf_op jit(solution)/shard_map/ppermute | solution.py:27
  16.5 11.9 %collective-permute-start.2 = (s32[3,16,1]{2,1,0:T(8,128)}, s32[3,16,1]{2,1,0:T(8,128)}, u32[]{:S(2)}, u32[]{:S(2)}) collective-permute-start(s32[3,16,1]{2,1,0:T(8,128)} %copy.30.mask_own), channel_id=1, source_target_pairs={{0,1},{1,0},{2,3},{3,2},{4,5},{5,4},{6,7},{7,6},{8,9},{9,8},{10,11... | collective-permute-start | bytes 584 | tf_op jit(solution)/shard_map/ppermute | solution.py:31
  28.4 9.7 %collective-permute-start.5 = (f32[3,256,128]{2,1,0:T(8,128)S(1)}, f32[3,256,128]{2,1,0:T(8,128)S(1)}, u32[]{:S(2)}, u32[]{:S(2)}) collective-permute-start(f32[3,256,128]{2,1,0:T(8,128)S(1)} %maximum_select_fusion.2.refs_0_), channel_id=1, source_target_pairs={{0,4},{1,17},{2,6},{3,19},{4,0},{5,21},{6,2},{7,23},{8,12},{9,25},... | collective-permute-start | bytes 1179656 | tf_op jit(solution)/shard_map/ppermute | solution.py:27
  31.4 11.1 %collective-permute-start.6 = (f32[3,256,128]{2,1,0:T(8,128)S(1)}, f32[3,256,128]{2,1,0:T(8,128)S(1)}, u32[]{:S(2)}, u32[]{:S(2)}) collective-permute-start(f32[3,256,128]{2,1,0:T(8,128)S(1)} %maximum_select_fusion.2.refs_0_), channel_id=1, source_target_pairs={{0,8},{1,3},{2,10},{3,5},{4,12},{5,7},{6,14},{7,1},{8,16},{9,11},{... | collective-permute-start | bytes 1179656 | tf_op jit(solution)/shard_map/ppermute | solution.py:27
  38.1 26.0 %copy-start.4 = (f32[3,256,128]{2,1,0:T(8,128)}, f32[3,256,128]{2,1,0:T(8,128)S(1)}, u32[]{:S(2)}) copy-start(f32[3,256,128]{2,1,0:T(8,128)S(1)} %collective-permute-done.5.refs_3_) | copy-start | bytes 1179652
  38.1 9.1 %collective-permute-start.7 = (f32[3,256,128]{2,1,0:T(8,128)S(1)}, f32[3,256,128]{2,1,0:T(8,128)S(1)}, u32[]{:S(2)}, u32[]{:S(2)}) collective-permute-start(f32[3,256,128]{2,1,0:T(8,128)S(1)} %maximum_select_fusion.2.refs_0_), channel_id=1, source_target_pairs={{0,24},{1,7},{2,26},{3,1},{4,28},{5,3},{6,30},{7,5},{8,0},{9,15},{... | collective-permute-start | bytes 1179656 | tf_op jit(solution)/shard_map/ppermute | solution.py:27
  42.5 29.8 %copy-start.5 = (f32[3,256,128]{2,1,0:T(8,128)}, f32[3,256,128]{2,1,0:T(8,128)S(1)}, u32[]{:S(2)}) copy-start(f32[3,256,128]{2,1,0:T(8,128)S(1)} %collective-permute-done.6.refs_4_) | copy-start | bytes 1179652
  42.5 8.3 %collective-permute-start.8 = (f32[3,256,128]{2,1,0:T(8,128)}, f32[3,256,128]{2,1,0:T(8,128)S(1)}, u32[]{:S(2)}, u32[]{:S(2)}) collective-permute-start(f32[3,256,128]{2,1,0:T(8,128)} %copy-done.3), channel_id=1, source_target_pairs={{0,8},{1,3},{2,10},{3,5},{4,12},{5,7},{6,14},{7,1},{8,16},{9,11},{... | collective-permute-start | bytes 1179656 | tf_op jit(solution)/shard_map/ppermute | solution.py:27
  47.2 28.3 %copy-start.6 = (f32[3,256,128]{2,1,0:T(8,128)}, f32[3,256,128]{2,1,0:T(8,128)S(1)}, u32[]{:S(2)}) copy-start(f32[3,256,128]{2,1,0:T(8,128)S(1)} %collective-permute-done.7.refs_5_) | copy-start | bytes 1179652
  47.2 8.4 %collective-permute-start.9 = (f32[3,256,128]{2,1,0:T(8,128)}, f32[3,256,128]{2,1,0:T(8,128)S(1)}, u32[]{:S(2)}, u32[]{:S(2)}) collective-permute-start(f32[3,256,128]{2,1,0:T(8,128)} %copy-done.3), channel_id=1, source_target_pairs={{0,24},{1,7},{2,26},{3,1},{4,28},{5,3},{6,30},{7,5},{8,0},{9,15},{... | collective-permute-start | bytes 1179656 | tf_op jit(solution)/shard_map/ppermute | solution.py:27
  50.8 25.6 %copy-start.7 = (f32[3,256,128]{2,1,0:T(8,128)}, f32[3,256,128]{2,1,0:T(8,128)S(1)}, u32[]{:S(2)}) copy-start(f32[3,256,128]{2,1,0:T(8,128)S(1)} %collective-permute-done.8.refs_6_) | copy-start | bytes 1179652
  50.8 8.4 %collective-permute-start.11 = (f32[3,256,128]{2,1,0:T(8,128)}, f32[3,256,128]{2,1,0:T(8,128)}, u32[]{:S(2)}, u32[]{:S(2)}) collective-permute-start(f32[3,256,128]{2,1,0:T(8,128)} %collective-permute-done.4.refs_2_), channel_id=1, source_target_pairs={{0,8},{1,3},{2,10},{3,5},{4,12},{5,7},{6,14},{7,1},{8,16},{9,11},{... | collective-permute-start | bytes 1179656 | tf_op jit(solution)/shard_map/ppermute | solution.py:27
  55.6 25.7 %copy-start.8 = (f32[3,256,128]{2,1,0:T(8,128)}, f32[3,256,128]{2,1,0:T(8,128)S(1)}, u32[]{:S(2)}) copy-start(f32[3,256,128]{2,1,0:T(8,128)S(1)} %collective-permute-done.9.refs_7_) | copy-start | bytes 1179652
  55.6 8.4 %collective-permute-start.12 = (f32[3,256,128]{2,1,0:T(8,128)}, f32[3,256,128]{2,1,0:T(8,128)S(1)}, u32[]{:S(2)}, u32[]{:S(2)}) collective-permute-start(f32[3,256,128]{2,1,0:T(8,128)} %collective-permute-done.4.refs_2_), channel_id=1, source_target_pairs={{0,24},{1,7},{2,26},{3,1},{4,28},{5,3},{6,30},{7,5},{8,0},{9,15},{... | collective-permute-start | bytes 1179656 | tf_op jit(solution)/shard_map/ppermute | solution.py:27
  59.3 8.2 %collective-permute-start.13 = (f32[3,256,128]{2,1,0:T(8,128)S(1)}, f32[3,256,128]{2,1,0:T(8,128)}, u32[]{:S(2)}, u32[]{:S(2)}) collective-permute-start(f32[3,256,128]{2,1,0:T(8,128)S(1)} %collective-permute-done.5.refs_3_), channel_id=1, source_target_pairs={{0,8},{1,3},{2,10},{3,5},{4,12},{5,7},{6,14},{7,1},{8,16},{9,11},{... | collective-permute-start | bytes 1179656 | tf_op jit(solution)/shard_map/ppermute | solution.py:27
  64.1 17.3 %copy-start.9 = (f32[3,256,128]{2,1,0:T(8,128)}, f32[3,256,128]{2,1,0:T(8,128)S(1)}, u32[]{:S(2)}) copy-start(f32[3,256,128]{2,1,0:T(8,128)S(1)} %collective-permute-done.12.refs_2_) | copy-start | bytes 1179652
  64.1 8.1 %collective-permute-start.14 = (f32[3,256,128]{2,1,0:T(8,128)S(1)}, f32[3,256,128]{2,1,0:T(8,128)}, u32[]{:S(2)}, u32[]{:S(2)}) collective-permute-start(f32[3,256,128]{2,1,0:T(8,128)S(1)} %collective-permute-done.5.refs_3_), channel_id=1, source_target_pairs={{0,24},{1,7},{2,26},{3,1},{4,28},{5,3},{6,30},{7,5},{8,0},{9,15},{... | collective-permute-start | bytes 1179656 | tf_op jit(solution)/shard_map/ppermute | solution.py:27
  67.5 8.9 %collective-permute-start.15 = (f32[3,256,128]{2,1,0:T(8,128)S(1)}, f32[3,256,128]{2,1,0:T(8,128)S(1)}, u32[]{:S(2)}, u32[]{:S(2)}) collective-permute-start(f32[3,256,128]{2,1,0:T(8,128)S(1)} %collective-permute-done.7.refs_5_), channel_id=1, source_target_pairs={{0,24},{1,7},{2,26},{3,1},{4,28},{5,3},{6,30},{7,5},{8,0},{9,15},{... | collective-permute-start | bytes 1179656 | tf_op jit(solution)/shard_map/ppermute | solution.py:27
  72.2 9.1 %collective-permute-start.16 = (f32[3,256,128]{2,1,0:T(8,128)S(1)}, f32[3,256,128]{2,1,0:T(8,128)S(1)}, u32[]{:S(2)}, u32[]{:S(2)}) collective-permute-start(f32[3,256,128]{2,1,0:T(8,128)S(1)} %collective-permute-done.9.refs_7_), channel_id=1, source_target_pairs={{0,24},{1,7},{2,26},{3,1},{4,28},{5,3},{6,30},{7,5},{8,0},{9,15},{... | collective-permute-start | bytes 1179656 | tf_op jit(solution)/shard_map/ppermute | solution.py:27
  76.4 5.0 %copy-start.10 = (f32[3,256,128]{2,1,0:T(8,128)}, f32[3,256,128]{2,1,0:T(8,128)S(1)}, u32[]{:S(2)}) copy-start(f32[3,256,128]{2,1,0:T(8,128)S(1)} %collective-permute-done.15.refs_0_) | copy-start | bytes 1179652
  76.5 76.8 %collective-permute-start.21 = (f32[3,128,2048]{2,1,0:T(8,128)}, f32[3,128,2048]{2,1,0:T(8,128)}, u32[]{:S(2)}, u32[]{:S(2)}) collective-permute-start(f32[3,128,2048]{2,1,0:T(8,128)} %bitcast.48), channel_id=1, source_target_pairs={{0,1},{1,0},{2,3},{3,2},{4,5},{5,4},{6,7},{7,6},{8,9},{9,8},{10,11... | collective-permute-start | bytes 9437192 | tf_op jit(solution)/shard_map/ppermute | solution.py:31
  81.4 16.7 %collective-permute-start.17 = (f32[3,256,128]{2,1,0:T(8,128)}, f32[3,256,128]{2,1,0:T(8,128)}, u32[]{:S(2)}, u32[]{:S(2)}) collective-permute-start(f32[3,256,128]{2,1,0:T(8,128)} %collective-permute-done.11.refs_1_), channel_id=1, source_target_pairs={{0,8},{1,3},{2,10},{3,5},{4,12},{5,7},{6,14},{7,1},{8,16},{9,11},{... | collective-permute-start | bytes 1179656 | tf_op jit(solution)/shard_map/ppermute | solution.py:27
  82.1 16.0 %collective-permute-start.18 = (f32[3,256,128]{2,1,0:T(8,128)}, f32[3,256,128]{2,1,0:T(8,128)}, u32[]{:S(2)}, u32[]{:S(2)}) collective-permute-start(f32[3,256,128]{2,1,0:T(8,128)} %collective-permute-done.14.refs_4_), channel_id=1, source_target_pairs={{0,24},{1,7},{2,26},{3,1},{4,28},{5,3},{6,30},{7,5},{8,0},{9,15},{... | collective-permute-start | bytes 1179656 | tf_op jit(solution)/shard_map/ppermute | solution.py:27
  98.1 22.2 %copy-start.22 = (f32[64,256]{1,0:T(8,128)S(1)}, f32[64,256]{1,0:T(8,128)}, u32[]{:S(2)}) copy-start(f32[64,256]{1,0:T(8,128)} %param.9) | copy-start | bytes 196612
  98.1 1.6 copy-start.1
  110.5 23.7 %all-to-all-start = ((f32[64,32,128]{2,1,0:T(8,128)}), f32[64,32,128]{2,1,0:T(8,128)S(1)}, u32[]{:S(2)}, u32[]{:S(2)}) async-start(f32[64,32,128]{2,1,0:T(8,128)} %bitcast.50), calls=%async_computation | async-start | bytes 2097152 | tf_op jit(solution)/shard_map/all_to_all | solution.py:332
  120.4 18.2 %collective-permute-start.20 = (f32[64,2048]{1,0:T(8,128)}, f32[64,2048]{1,0:T(8,128)S(1)}, u32[]{:S(2)}, u32[]{:S(2)}) collective-permute-start(f32[64,2048]{1,0:T(8,128)} %param.15), channel_id=1, source_target_pairs={{0,1},{1,0},{2,3},{3,2},{4,5},{5,4},{6,7},{7,6},{8,9},{9,8},{10,11... | collective-permute-start | bytes 1572872 | tf_op jit(solution)/shard_map/ppermute | solution.py:31
  126.2 8.1 %collective-permute-start.1 = (f32[64,128]{0,1:T(8,128)S(1)}, f32[64,128]{0,1:T(8,128)S(1)}, u32[]{:S(2)}, u32[]{:S(2)}) collective-permute-start(f32[64,128]{0,1:T(8,128)S(1)} %get-tuple-element.35), channel_id=1, source_target_pairs={{0,1},{1,0},{2,3},{3,2},{4,5},{5,4},{6,7},{7,6},{8,9},{9,8},{10,11... | collective-permute-start | bytes 98312 | tf_op jit(solution)/shard_map/ppermute | solution.py:31
  135.1 11.0 %all-to-all-start.1 = ((f32[16,32,128]{2,1,0:T(8,128)}), f32[16,32,128]{2,1,0:T(8,128)S(1)}, u32[]{:S(2)}, u32[]{:S(2)}) async-start(f32[16,32,128]{2,1,0:T(8,128)} %broadcast_in_dim.8), calls=%async_computation.1 | async-start | bytes 524288 | tf_op jit(solution)/shard_map/all_to_all | solution.py:337
  148.4 18.5 %all-to-all-start.2 = ((f32[64,32,128]{2,1,0:T(8,128)}), f32[64,32,128]{2,1,0:T(8,128)S(1)}, u32[]{:S(2)}, u32[]{:S(2)}) async-start(f32[64,32,128]{2,1,0:T(8,128)} %broadcast_in_dim.18), calls=%async_computation.2 | async-start | bytes 2097152 | tf_op jit(solution)/shard_map/all_to_all | solution.py:344
  166.9 1.0 copy-start
  174.7 6.9 %collective-permute-start.22 = (f32[3,256,128]{2,1,0:T(8,128)}, f32[3,256,128]{2,1,0:T(8,128)S(1)}, u32[]{:S(2)}, u32[]{:S(2)}) collective-permute-start(f32[3,256,128]{2,1,0:T(8,128)} %shard_map.99.refs_0_), channel_id=1, source_target_pairs={{0,6},{1,25},{2,0},{3,27},{4,2},{5,29},{6,4},{7,31},{8,14},{9,1},{... | collective-permute-start | bytes 1179656 | tf_op jit(solution)/shard_map/ppermute | solution.py:27
  174.9 12.3 %collective-permute-start.23 = (f32[3,256,128]{2,1,0:T(8,128)}, f32[3,256,128]{2,1,0:T(8,128)S(1)}, u32[]{:S(2)}, u32[]{:S(2)}) collective-permute-start(f32[3,256,128]{2,1,0:T(8,128)} %shard_map.99.refs_0_), channel_id=1, source_target_pairs={{0,2},{1,9},{2,4},{3,11},{4,6},{5,13},{6,0},{7,15},{8,10},{9,17},{... | collective-permute-start | bytes 1179656 | tf_op jit(solution)/shard_map/ppermute | solution.py:27
  176.3 11.7 %collective-permute-start.24 = (f32[3,256,128]{2,1,0:T(8,128)}, f32[3,256,128]{2,1,0:T(8,128)S(1)}, u32[]{:S(2)}, u32[]{:S(2)}) collective-permute-start(f32[3,256,128]{2,1,0:T(8,128)} %shard_map.99.refs_0_), channel_id=1, source_target_pairs={{0,4},{1,17},{2,6},{3,19},{4,0},{5,21},{6,2},{7,23},{8,12},{9,25},... | collective-permute-start | bytes 1179656 | tf_op jit(solution)/shard_map/ppermute | solution.py:27
  176.9 11.7 %collective-permute-start.25 = (f32[3,256,128]{2,1,0:T(8,128)}, f32[3,256,128]{2,1,0:T(8,128)S(1)}, u32[]{:S(2)}, u32[]{:S(2)}) collective-permute-start(f32[3,256,128]{2,1,0:T(8,128)} %shard_map.99.refs_0_), channel_id=1, source_target_pairs={{0,8},{1,3},{2,10},{3,5},{4,12},{5,7},{6,14},{7,1},{8,16},{9,11},{... | collective-permute-start | bytes 1179656 | tf_op jit(solution)/shard_map/ppermute | solution.py:27
  177.2 13.4 %collective-permute-start.26 = (f32[3,256,128]{2,1,0:T(8,128)}, f32[3,256,128]{2,1,0:T(8,128)S(1)}, u32[]{:S(2)}, u32[]{:S(2)}) collective-permute-start(f32[3,256,128]{2,1,0:T(8,128)} %shard_map.99.refs_0_), channel_id=1, source_target_pairs={{0,24},{1,7},{2,26},{3,1},{4,28},{5,3},{6,30},{7,5},{8,0},{9,15},{... | collective-permute-start | bytes 1179656 | tf_op jit(solution)/shard_map/ppermute | solution.py:27
  181.6 29.0 %copy-start.11 = (f32[3,256,128]{2,1,0:T(8,128)}, f32[3,256,128]{2,1,0:T(8,128)S(1)}, u32[]{:S(2)}) copy-start(f32[3,256,128]{2,1,0:T(8,128)S(1)} %collective-permute-done.22.refs_1_) | copy-start | bytes 1179652
  181.6 9.1 %collective-permute-start.27 = (f32[3,256,128]{2,1,0:T(8,128)S(1)}, f32[3,256,128]{2,1,0:T(8,128)S(1)}, u32[]{:S(2)}, u32[]{:S(2)}) collective-permute-start(f32[3,256,128]{2,1,0:T(8,128)S(1)} %collective-permute-done.22.refs_1_), channel_id=1, source_target_pairs={{0,8},{1,3},{2,10},{3,5},{4,12},{5,7},{6,14},{7,1},{8,16},{9,11},{... | collective-permute-start | bytes 1179656 | tf_op jit(solution)/shard_map/ppermute | solution.py:27
  187.1 23.5 %copy-start.13 = (f32[3,256,128]{2,1,0:T(8,128)}, f32[3,256,128]{2,1,0:T(8,128)S(1)}, u32[]{:S(2)}) copy-start(f32[3,256,128]{2,1,0:T(8,128)S(1)} %collective-permute-done.23.refs_2_) | copy-start | bytes 1179652
  187.1 11.1 %collective-permute-start.28 = (f32[3,256,128]{2,1,0:T(8,128)S(1)}, f32[3,256,128]{2,1,0:T(8,128)S(1)}, u32[]{:S(2)}, u32[]{:S(2)}) collective-permute-start(f32[3,256,128]{2,1,0:T(8,128)S(1)} %collective-permute-done.22.refs_1_), channel_id=1, source_target_pairs={{0,24},{1,7},{2,26},{3,1},{4,28},{5,3},{6,30},{7,5},{8,0},{9,15},{... | collective-permute-start | bytes 1179656 | tf_op jit(solution)/shard_map/ppermute | solution.py:27
  187.9 22.7 %copy-start.14 = (f32[3,256,128]{2,1,0:T(8,128)}, f32[3,256,128]{2,1,0:T(8,128)S(1)}, u32[]{:S(2)}) copy-start(f32[3,256,128]{2,1,0:T(8,128)S(1)} %collective-permute-done.24.refs_3_) | copy-start | bytes 1179652
  187.9 13.2 %collective-permute-start.30 = (f32[3,256,128]{2,1,0:T(8,128)S(1)}, f32[3,256,128]{2,1,0:T(8,128)S(1)}, u32[]{:S(2)}, u32[]{:S(2)}) collective-permute-start(f32[3,256,128]{2,1,0:T(8,128)S(1)} %collective-permute-done.23.refs_2_), channel_id=1, source_target_pairs={{0,8},{1,3},{2,10},{3,5},{4,12},{5,7},{6,14},{7,1},{8,16},{9,11},{... | collective-permute-start | bytes 1179656 | tf_op jit(solution)/shard_map/ppermute | solution.py:27
  188.6 22.0 %copy-start.16 = (f32[3,256,128]{2,1,0:T(8,128)}, f32[3,256,128]{2,1,0:T(8,128)S(1)}, u32[]{:S(2)}) copy-start(f32[3,256,128]{2,1,0:T(8,128)S(1)} %collective-permute-done.25.refs_4_) | copy-start | bytes 1179652
  188.6 15.1 %collective-permute-start.31 = (f32[3,256,128]{2,1,0:T(8,128)S(1)}, f32[3,256,128]{2,1,0:T(8,128)S(1)}, u32[]{:S(2)}, u32[]{:S(2)}) collective-permute-start(f32[3,256,128]{2,1,0:T(8,128)S(1)} %collective-permute-done.23.refs_2_), channel_id=1, source_target_pairs={{0,24},{1,7},{2,26},{3,1},{4,28},{5,3},{6,30},{7,5},{8,0},{9,15},{... | collective-permute-start | bytes 1179656 | tf_op jit(solution)/shard_map/ppermute | solution.py:27
  190.6 20.1 %copy-start.15 = (f32[3,256,128]{2,1,0:T(8,128)}, f32[3,256,128]{2,1,0:T(8,128)S(1)}, u32[]{:S(2)}) copy-start(f32[3,256,128]{2,1,0:T(8,128)S(1)} %collective-permute-done.26.refs_5_) | copy-start | bytes 1179652
  190.6 17.0 %collective-permute-start.33 = (f32[3,256,128]{2,1,0:T(8,128)S(1)}, f32[3,256,128]{2,1,0:T(8,128)S(1)}, u32[]{:S(2)}, u32[]{:S(2)}) collective-permute-start(f32[3,256,128]{2,1,0:T(8,128)S(1)} %collective-permute-done.24.refs_3_), channel_id=1, source_target_pairs={{0,24},{1,7},{2,26},{3,1},{4,28},{5,3},{6,30},{7,5},{8,0},{9,15},{... | collective-permute-start | bytes 1179656 | tf_op jit(solution)/shard_map/ppermute | solution.py:27
  190.7 20.0 %copy-start.19 = (f32[3,256,128]{2,1,0:T(8,128)}, f32[3,256,128]{2,1,0:T(8,128)S(1)}, u32[]{:S(2)}) copy-start(f32[3,256,128]{2,1,0:T(8,128)S(1)} %collective-permute-done.27.refs_6_) | copy-start | bytes 1179652
  190.7 27.5 %collective-permute-start.32 = (f32[3,256,128]{2,1,0:T(8,128)S(1)}, f32[3,256,128]{2,1,0:T(8,128)}, u32[]{:S(2)}, u32[]{:S(2)}) collective-permute-start(f32[3,256,128]{2,1,0:T(8,128)S(1)} %collective-permute-done.24.refs_3_), channel_id=1, source_target_pairs={{0,8},{1,3},{2,10},{3,5},{4,12},{5,7},{6,14},{7,1},{8,16},{9,11},{... | collective-permute-start | bytes 1179656 | tf_op jit(solution)/shard_map/ppermute | solution.py:27
  198.3 12.4 %copy-start.17 = (f32[3,256,128]{2,1,0:T(8,128)}, f32[3,256,128]{2,1,0:T(8,128)S(1)}, u32[]{:S(2)}) copy-start(f32[3,256,128]{2,1,0:T(8,128)S(1)} %collective-permute-done.28.refs_7_) | copy-start | bytes 1179652
  198.3 25.4 %collective-permute-start.34 = (f32[3,256,128]{2,1,0:T(8,128)S(1)}, f32[3,256,128]{2,1,0:T(8,128)}, u32[]{:S(2)}, u32[]{:S(2)}) collective-permute-start(f32[3,256,128]{2,1,0:T(8,128)S(1)} %collective-permute-done.26.refs_5_), channel_id=1, source_target_pairs={{0,24},{1,7},{2,26},{3,1},{4,28},{5,3},{6,30},{7,5},{8,0},{9,15},{... | collective-permute-start | bytes 1179656 | tf_op jit(solution)/shard_map/ppermute | solution.py:27
  201.1 17.1 %copy-start.18 = (f32[3,256,128]{2,1,0:T(8,128)}, f32[3,256,128]{2,1,0:T(8,128)S(1)}, u32[]{:S(2)}) copy-start(f32[3,256,128]{2,1,0:T(8,128)S(1)} %collective-permute-done.30.refs_1_) | copy-start | bytes 1179652
  201.1 22.5 %collective-permute-start.35 = (f32[3,256,128]{2,1,0:T(8,128)S(1)}, f32[3,256,128]{2,1,0:T(8,128)}, u32[]{:S(2)}, u32[]{:S(2)}) collective-permute-start(f32[3,256,128]{2,1,0:T(8,128)S(1)} %collective-permute-done.28.refs_7_), channel_id=1, source_target_pairs={{0,24},{1,7},{2,26},{3,1},{4,28},{5,3},{6,30},{7,5},{8,0},{9,15},{... | collective-permute-start | bytes 1179656 | tf_op jit(solution)/shard_map/ppermute | solution.py:27
  203.7 3.9 %copy-start.21 = (f32[3,256,128]{2,1,0:T(8,128)}, f32[3,256,128]{2,1,0:T(8,128)S(1)}, u32[]{:S(2)}) copy-start(f32[3,256,128]{2,1,0:T(8,128)S(1)} %collective-permute-done.31.refs_2_) | copy-start | bytes 1179652
  203.7 19.9 %collective-permute-start.36 = (f32[3,256,128]{2,1,0:T(8,128)S(1)}, f32[3,256,128]{2,1,0:T(8,128)}, u32[]{:S(2)}, u32[]{:S(2)}) collective-permute-start(f32[3,256,128]{2,1,0:T(8,128)S(1)} %collective-permute-done.30.refs_1_), channel_id=1, source_target_pairs={{0,8},{1,3},{2,10},{3,5},{4,12},{5,7},{6,14},{7,1},{8,16},{9,11},{... | collective-permute-start | bytes 1179656 | tf_op jit(solution)/shard_map/ppermute | solution.py:27
  207.6 10.5 %copy-start.20 = (f32[3,256,128]{2,1,0:T(8,128)}, f32[3,256,128]{2,1,0:T(8,128)S(1)}, u32[]{:S(2)}) copy-start(f32[3,256,128]{2,1,0:T(8,128)S(1)} %collective-permute-done.33.refs_4_) | copy-start | bytes 1179652
  207.6 16.0 %collective-permute-start.37 = (f32[3,256,128]{2,1,0:T(8,128)S(1)}, f32[3,256,128]{2,1,0:T(8,128)}, u32[]{:S(2)}, u32[]{:S(2)}) collective-permute-start(f32[3,256,128]{2,1,0:T(8,128)S(1)} %collective-permute-done.33.refs_4_), channel_id=1, source_target_pairs={{0,24},{1,7},{2,26},{3,1},{4,28},{5,3},{6,30},{7,5},{8,0},{9,15},{... | collective-permute-start | bytes 1179656 | tf_op jit(solution)/shard_map/ppermute | solution.py:27
  229.1 13.0 %collective-permute-start.38 = (f32[3,128,128]{2,1,0:T(8,128)}, f32[3,128,128]{2,1,0:T(8,128)S(1)}, u32[]{:S(2)}, u32[]{:S(2)}) collective-permute-start(f32[3,128,128]{2,1,0:T(8,128)} %get-tuple-element.27), channel_id=1, source_target_pairs={{0,1},{1,0},{2,3},{3,2},{4,5},{5,4},{6,7},{7,6},{8,9},{9,8},{10,11... | collective-permute-start | bytes 589832 | tf_op jit(solution)/shard_map/ppermute | solution.py:31
  240.1 1.3 collective-permute-start.39
  (2 other events, 1.5 us)
where the time goes:
time: 244 us; the launch traced here: 243 us
  starting transfers between devices  86.6 us (35%)
  waiting for transfers between devices  85.9 us (35%)
  Pallas kernels  56.1 us (23%)
  local copies, waits for them, and re-layouts  10.1 us (4%)
    ppermute x30, waiting for transfers between devices, shift(): return lax.ppermute(array, 'row', pairs)  51.1 us
    ppermute x30, starting transfers between devices, shift(): return lax.ppermute(array, 'row', pairs)  43.3 us
    pallas_call x4, Pallas kernels, run_add(): pl.pallas_call(functools.partial(add_kernel, stage, total is not None), o...  25.8 us
    ppermute x10, starting transfers between devices, swap(): return lax.ppermute(array, 'row', [(i, i ^ 1) for i in range(32)])  25 us
    ppermute x10, waiting for transfers between devices, swap(): return lax.ppermute(array, 'row', [(i, i ^ 1) for i in range(32)])  14.2 us
    pallas_call x1, Pallas kernels, run_lower(): pl.pallas_call(functools.partial(lower_kernel, len(pieces)), out_shape=(s...  10.7 us
    all_to_all x1, starting transfers between devices, body(): lax.all_to_all(parts.reshape(64, 32, 128), ('layer', 'row'), 0, 0, tiled=...  9.83 us
    all_to_all x1, waiting for transfers between devices, body(): lax.all_to_all(jnp.broadcast_to(reduced[None], (CH, 32, 128)), 'row', 0,...  7.44 us
  transfers between devices with their start and end apart: 43, of which 21 were waited for; matrix products, arithmetic and copies ran while one was open for 3% of the time, Pallas kernels for 21%

commit v1 on v0

--- a/solution.py
+++ b/solution.py
@@ -34,8 +34,8 @@
 SAME_CORE = [[2 * i + c for i in range(CH)] for c in range(2)]
 SAME_CORE_ALL = [[l * 32 + 2 * i + c for l in range(4) for i in range(CH)] for c in range(2)]
 
-FIRST = [(0, 0), (1, 0), (-1, 0), (2, 0), (0, -1), (0, 1), (1, -1), (1, 1)]
-SECOND = [(-1, -1), (-1, 1), (2, -1), (2, 1)]
+FIRST = [(0, 0), (1, 0), (-1, 0), (2, 0)]
+SECOND = [(0, -1), (0, 1), (1, -1), (1, 1), (-1, -1), (-1, 1), (2, -1), (2, 1)]
 LATE = [(0, 2), (1, 2), (-1, 2), (2, 2)]
 
 
@@ -48,8 +48,8 @@
         ups.append(move(value, 0, 1))
         downs.append(move(value, 0, -1))
     late = [move(downs[0], 0, -1), move(downs[1], 0, -1), move(ups[2], 0, 1), move(downs[3], 0, -1)]
-    first = [own, right, left, far, ups[0], downs[0], ups[1], downs[1]]
-    return first, [ups[2], downs[2], ups[3], downs[3]], late
+    second = [piece for pair in zip(ups, downs) for piece in pair]
+    return [own, right, left, far], second, late
 
 
 def halves(value):
@@ -170,18 +170,14 @@
         out_part[k] = value[128:]
 
 
-def couple_kernel(pos, root, interim, up, residue, up_v, w, sems):
-    copies = [pltpu.make_async_copy(up.at[k], up_v.at[k], sems.at[k]) for k in range(K)]
-    for copy in copies:
-        copy.start()
+def couple_kernel(pos, root, interim, up, residue, w):
     for i in range(CH):
         flat = jnp.concatenate([root[z, i] for z in range(4)], axis=0)
         w[i * 128 : i * 128 + 128, :] = stacked(flat.T, 1)
     here = pl.ds(pl.multiple_of(pos[2] * 128, 128), 128)
     there = pl.ds(pl.multiple_of((1 - pos[2]) * 128, 128), 128)
     for k in range(K):
-        copies[k].wait()
-        value = interim[k] - product(up_v[k], w[...])
+        value = interim[k] - product(up[k], w[...])
         residue[k, here, :] = value[:128]
         residue[k, there, :] = value[128:]
 
@@ -196,7 +192,7 @@
             out[0, 256 + n * 128 : 384 + n * 128, lanes] = low
 
 
-BIG = 58
+BIG = 63.5
 VMEM = pl.BlockSpec(memory_space=pltpu.VMEM)
 HBM = pl.BlockSpec(memory_space=pltpu.HBM)
 SMEM = pl.BlockSpec(memory_space=pltpu.SMEM)
@@ -207,7 +203,7 @@
 
 
 def limit(mib):
-    return pltpu.CompilerParams(vmem_limit_bytes=mib * 1024 * 1024)
+    return pltpu.CompilerParams(vmem_limit_bytes=int(mib * 1024 * 1024))
 
 
 def stage_scratch(stage, pieces):
@@ -265,14 +261,10 @@
     return pl.pallas_call(
         couple_kernel,
         out_shape=sds(K, 256, 128),
-        in_specs=[SMEM, VMEM, VMEM, HBM],
+        in_specs=[SMEM, VMEM, VMEM, VMEM],
         out_specs=VMEM,
-        scratch_shapes=[
-            pltpu.VMEM((K, 512, 2048), BF16),
-            pltpu.VMEM((2048, 256), BF16),
-            pltpu.SemaphoreType.DMA((K,)),
-        ],
-        compiler_params=limit(BIG),
+        scratch_shapes=[pltpu.VMEM((2048, 256), BF16)],
+        compiler_params=limit(36),
     )(pos, root, interim, up)
 
 
@@ -280,11 +272,11 @@
     block = pl.BlockSpec((1, 128, 2048), lambda k: (k, 0, 0))
     return pl.pallas_call(
         up_kernel,
-        out_shape=pltpu.HBM((K, 512, 2048), BF16),
+        out_shape=pltpu.VMEM((K, 512, 2048), BF16),
         grid=(K,),
         in_specs=[SMEM, SMEM, block, block],
         out_specs=pl.BlockSpec((1, 512, 2048), lambda k: (k, 0, 0)),
-        compiler_params=limit(BIG),
+        compiler_params=limit(36),
     )(mask_own, mask_part, own, part)
 
 

time: 244 us -> 238 us (0.975)
  Pallas kernels: 56.1 us -> 48.2 us
  local copies, waits for them, and re-layouts: 10.1 us -> 13.4 us
  starting transfers between devices: 86.6 us -> 83.3 us
  waiting for transfers between devices: 85.9 us -> 88.5 us
    unnamed x47 -> x55, local copies, waits for them, and re-layouts: 4.1 us -> 8.78 us
    pallas_call x1, Pallas kernels: 6.85 us -> 2.44 us  [run_couple(): pl.pallas_call(couple_kernel, out_shape=sds(K, 256, 128), in_specs=[SMEM,...]
    pallas_call x1, Pallas kernels: 7.34 us -> 3.79 us  [run_up(): pl.pallas_call(up_kernel, out_shape=pltpu.VMEM((K, 512, 2048), BF16), gri...]
    ppermute x30, starting transfers between devices: 43.3 us -> 39.8 us  [shift(): return lax.ppermute(array, 'row', pairs)]
  transfers between devices with their start and end apart: 43 -> 43, of which waited for: 21 -> 23; matrix products, arithmetic and copies ran while one was open for 3% -> 3% of each run, Pallas kernels for 21% -> 18%
where the time goes in v1:
time: 238 us
  waiting for transfers between devices  88.5 us (37%)
  starting transfers between devices  83.3 us (35%)
  Pallas kernels  48.2 us (20%)
  local copies, waits for them, and re-layouts  13.4 us (6%)
    ppermute x30, waiting for transfers between devices, shift(): return lax.ppermute(array, 'row', pairs)  52.8 us
    ppermute x30, starting transfers between devices, shift(): return lax.ppermute(array, 'row', pairs)  39.8 us
    pallas_call x4, Pallas kernels, run_add(): pl.pallas_call(functools.partial(add_kernel, stage, total is not None), o...  25.8 us
    ppermute x10, starting transfers between devices, swap(): return lax.ppermute(array, 'row', [(i, i ^ 1) for i in range(32)])  25 us
    ppermute x10, waiting for transfers between devices, swap(): return lax.ppermute(array, 'row', [(i, i ^ 1) for i in range(32)])  15.1 us
    pallas_call x1, Pallas kernels, run_lower(): pl.pallas_call(functools.partial(lower_kernel, len(pieces)), out_shape=(s...  10.7 us
    all_to_all x1, starting transfers between devices, body(): lax.all_to_all(parts.reshape(64, 32, 128), ('layer', 'row'), 0, 0, tiled=...  10.1 us
    unnamed x55, local copies, waits for them, and re-layouts  8.78 us
  transfers between devices with their start and end apart: 43, of which 23 were waited for; matrix products, arithmetic and copies ran while one was open for 3% of the time, Pallas kernels for 18%

profile of v1, /device:TPU:1, one launch (start us, length us, event | category | flops | bytes accessed | tf_op | source)
XLA Modules:
  0.0 237.7 jit_solution(6130191433982704973)
XLA Ops:
  0.6 1.1 slice_select_fusion.1
  1.7 1.5 collective-permute-start
  3.2 1.1 collective-permute-done
  4.7 2.8 %collective-permute-start.3 = (f32[3,256,128]{2,1,0:T(8,128)S(1)}, f32[3,256,128]{2,1,0:T(8,128)S(1)}, u32[]{:S(2)}, u32[]{:S(2)}) collective-permute-start(f32[3,256,128]{2,1,0:T(8,128)S(1)} %maximum_select_fusion.2.refs_0_), channel_id=1, source_target_pairs={{0,6},{1,25},{2,0},{3,27},{4,2},{5,29},{6,4},{7,31},{8,14},{9,1},{... | collective-permute-start | bytes 1179656 | tf_op jit(solution)/shard_map/ppermute | solution.py:27
  7.6 4.7 %collective-permute-done.3.refs_1_ = f32[3,256,128]{2,1,0:T(8,128)S(1)} collective-permute-done((f32[3,256,128]{2,1,0:T(8,128)S(1)}, f32[3,256,128]{2,1,0:T(8,128)S(1)}, u32[]{:S(2)}, u32[]{:S(2)}) %collective-permute-start.3) | collective-permute-done | bytes 393248 | tf_op jit(solution)/shard_map/ppermute | solution.py:27
  12.3 0.7 collective-permute-start.25
  13.0 1.3 collective-permute-start.4
  14.3 0.8 copy.30.mask_own
  15.6 12.8 %collective-permute-done.2.mask_part = s32[3,16,1]{2,1,0:T(8,128)S(1)} collective-permute-done((s32[3,16,1]{2,1,0:T(8,128)S(1)}, s32[3,16,1]{2,1,0:T(8,128)S(1)}, u32[]{:S(2)}, u32[]{:S(2)}) %collective-permute-start.2) | collective-permute-done | bytes 224 | tf_op jit(solution)/shard_map/ppermute | solution.py:31
  28.4 3.0 %collective-permute-start.5 = (f32[3,256,128]{2,1,0:T(8,128)S(1)}, f32[3,256,128]{2,1,0:T(8,128)S(1)}, u32[]{:S(2)}, u32[]{:S(2)}) collective-permute-start(f32[3,256,128]{2,1,0:T(8,128)S(1)} %maximum_select_fusion.2.refs_0_), channel_id=1, source_target_pairs={{0,4},{1,17},{2,6},{3,19},{4,0},{5,21},{6,2},{7,23},{8,12},{9,25},... | collective-permute-start | bytes 1179656 | tf_op jit(solution)/shard_map/ppermute | solution.py:27
  31.4 1.2 collective-permute-start.7
  32.6 5.5 %collective-permute-done.5.refs_3_ = f32[3,256,128]{2,1,0:T(8,128)S(1)} collective-permute-done((f32[3,256,128]{2,1,0:T(8,128)S(1)}, f32[3,256,128]{2,1,0:T(8,128)S(1)}, u32[]{:S(2)}, u32[]{:S(2)}) %collective-permute-start.5) | collective-permute-done | bytes 393248 | tf_op jit(solution)/shard_map/ppermute | solution.py:27
  38.1 4.4 %collective-permute-start.8 = (f32[3,256,128]{2,1,0:T(8,128)S(1)}, f32[3,256,128]{2,1,0:T(8,128)S(1)}, u32[]{:S(2)}, u32[]{:S(2)}) collective-permute-start(f32[3,256,128]{2,1,0:T(8,128)S(1)} %maximum_select_fusion.2.refs_0_), channel_id=1, source_target_pairs={{0,24},{1,7},{2,26},{3,1},{4,28},{5,3},{6,30},{7,5},{8,0},{9,15},{... | collective-permute-start | bytes 1179656 | tf_op jit(solution)/shard_map/ppermute | solution.py:27
  43.1 4.1 %collective-permute-done.8.refs_2_ = f32[3,256,128]{2,1,0:T(8,128)S(1)} collective-permute-done((f32[3,256,128]{2,1,0:T(8,128)S(1)}, f32[3,256,128]{2,1,0:T(8,128)S(1)}, u32[]{:S(2)}, u32[]{:S(2)}) %collective-permute-start.8) | collective-permute-done | bytes 393248 | tf_op jit(solution)/shard_map/ppermute | solution.py:27
  47.2 0.8 collective-permute-start.11
  47.9 3.4 %collective-permute-done.10.refs_4_ = f32[3,256,128]{2,1,0:T(8,128)S(1)} collective-permute-done((f32[3,256,128]{2,1,0:T(8,128)S(1)}, f32[3,256,128]{2,1,0:T(8,128)S(1)}, u32[]{:S(2)}, u32[]{:S(2)}) %collective-permute-start.10) | collective-permute-done | bytes 393248 | tf_op jit(solution)/shard_map/ppermute | solution.py:27
  51.4 3.5 %collective-permute-start.12 = (f32[3,256,128]{2,1,0:T(8,128)S(1)}, f32[3,256,128]{2,1,0:T(8,128)S(1)}, u32[]{:S(2)}, u32[]{:S(2)}) collective-permute-start(f32[3,256,128]{2,1,0:T(8,128)S(1)} %collective-permute-done.4.refs_2_), channel_id=1, source_target_pairs={{0,24},{1,7},{2,26},{3,1},{4,28},{5,3},{6,30},{7,5},{8,0},{9,15},{... | collective-permute-start | bytes 1179656 | tf_op jit(solution)/shard_map/ppermute | solution.py:27
  54.9 1.0 collective-permute-done.11.refs_5_
  55.8 3.8 %collective-permute-done.12.refs_6_ = f32[3,256,128]{2,1,0:T(8,128)S(1)} collective-permute-done((f32[3,256,128]{2,1,0:T(8,128)S(1)}, f32[3,256,128]{2,1,0:T(8,128)S(1)}, u32[]{:S(2)}, u32[]{:S(2)}) %collective-permute-start.12) | collective-permute-done | bytes 393248 | tf_op jit(solution)/shard_map/ppermute | solution.py:27
  59.6 3.4 %collective-permute-start.14 = (f32[3,256,128]{2,1,0:T(8,128)S(1)}, f32[3,256,128]{2,1,0:T(8,128)}, u32[]{:S(2)}, u32[]{:S(2)}) collective-permute-start(f32[3,256,128]{2,1,0:T(8,128)S(1)} %collective-permute-done.5.refs_3_), channel_id=1, source_target_pairs={{0,24},{1,7},{2,26},{3,1},{4,28},{5,3},{6,30},{7,5},{8,0},{9,15},{... | collective-permute-start | bytes 1179656 | tf_op jit(solution)/shard_map/ppermute | solution.py:27
  63.0 0.9 collective-permute-done.13.refs_7_
  64.0 3.8 %collective-permute-done.14.refs_8_ = f32[3,256,128]{2,1,0:T(8,128)} collective-permute-done((f32[3,256,128]{2,1,0:T(8,128)S(1)}, f32[3,256,128]{2,1,0:T(8,128)}, u32[]{:S(2)}, u32[]{:S(2)}) %collective-permute-start.14) | collective-permute-done | bytes 393248 | tf_op jit(solution)/shard_map/ppermute | solution.py:27
  67.7 3.2 %collective-permute-start.15 = (f32[3,256,128]{2,1,0:T(8,128)S(1)}, f32[3,256,128]{2,1,0:T(8,128)S(1)}, u32[]{:S(2)}, u32[]{:S(2)}) collective-permute-start(f32[3,256,128]{2,1,0:T(8,128)S(1)} %collective-permute-done.8.refs_2_), channel_id=1, source_target_pairs={{0,24},{1,7},{2,26},{3,1},{4,28},{5,3},{6,30},{7,5},{8,0},{9,15},{... | collective-permute-start | bytes 1179656 | tf_op jit(solution)/shard_map/ppermute | solution.py:27
  71.0 1.0 collective-permute-done.9.refs_3_
  71.9 3.8 %collective-permute-done.15.refs_0_ = f32[3,256,128]{2,1,0:T(8,128)S(1)} collective-permute-done((f32[3,256,128]{2,1,0:T(8,128)S(1)}, f32[3,256,128]{2,1,0:T(8,128)S(1)}, u32[]{:S(2)}, u32[]{:S(2)}) %collective-permute-start.15) | collective-permute-done | bytes 393248 | tf_op jit(solution)/shard_map/ppermute | solution.py:27
  75.7 5.3 %collective-permute-start.21 = (f32[3,128,2048]{2,1,0:T(8,128)}, f32[3,128,2048]{2,1,0:T(8,128)}, u32[]{:S(2)}, u32[]{:S(2)}) collective-permute-start(f32[3,128,2048]{2,1,0:T(8,128)} %bitcast.38), channel_id=1, source_target_pairs={{0,1},{1,0},{2,3},{3,2},{4,5},{5,4},{6,7},{7,6},{8,9},{9,8},{10,11... | collective-permute-start | bytes 9437192 | tf_op jit(solution)/shard_map/ppermute | solution.py:31
  81.8 2.3 collective-permute-start.18
  84.7 5.1 %shard_map.95.refs_0_ = f32[3,256,128]{2,1,0:T(8,128)} custom-call(s32[3]{0:T(128)} %pad_add_fusion.pos, f32[3,256,128]{2,1,0:T(8,128)} %copy-done.10, f32[3,256,128]{2,1,0:T(8,128)} %copy-done.11, f32[3,256,128]{2,1,0:T(8,128)} %copy-done.12, f32[3,256,128]{2,1,0:T(8,128)} %copy-done.13, f32[3,128,4096]{2,1,0:T(8,128)} %bitcast.41, ...), custom_call_target="tpu_custom_call" | custom-call | tf_op jit(solution)/shard_map/pallas_call | solution.py:221
  89.8 7.8 %shard_map.96.total = f32[3,256,128]{2,1,0:T(8,128)} custom-call(s32[3]{0:T(128)} %pad_add_fusion.pos, f32[3,256,128]{2,1,0:T(8,128)} %shard_map.95.refs_0_, f32[3,256,128]{2,1,0:T(8,128)} %copy-done.14, f32[3,256,128]{2,1,0:T(8,128)} %copy-done.15, f32[3,256,128]{2,1,0:T(8,128)} %collective-permute-done.9.refs_3_, f32[3,256,128]{2,1,0:T(8,128)} %copy-done.16, ...), custom_call_target="tpu_custom_call" | custom-call | tf_op jit(solution)/shard_map/pallas_call | solution.py:221
  97.7 10.7 %shard_map.97 = (f32[3,256,128]{2,1,0:T(8,128)}, f32[4,16,32,128]{3,2,1,0:T(8,128)}) custom-call(s32[3]{0:T(128)} %pad_add_fusion.pos, s32[3,16,1]{2,1,0:T(8,128)} %copy-done.5, s32[3,16,1]{2,1,0:T(8,128)} %copy-done.7, f32[3,256,128]{2,1,0:T(8,128)} %shard_map.96.total, f32[3,256,128]{2,1,0:T(8,128)} %copy-done.19, f32[3,256,128]{2,1,0:T(8,128)} %copy-done.21, ...), custom_call_target="tpu_custom_call" | custom-call | tf_op jit(solution)/shard_map/pallas_call | solution.py:233
  108.5 10.1 %all-to-all-start = ((f32[64,32,128]{2,1,0:T(8,128)}), f32[64,32,128]{2,1,0:T(8,128)S(1)}, u32[]{:S(2)}, u32[]{:S(2)}) async-start(f32[64,32,128]{2,1,0:T(8,128)} %bitcast.50), calls=%async_computation | async-start | bytes 2097152 | tf_op jit(solution)/shard_map/all_to_all | solution.py:324
  118.7 5.0 %collective-permute-start.20 = (f32[64,2048]{1,0:T(8,128)}, f32[64,2048]{1,0:T(8,128)S(1)}, u32[]{:S(2)}, u32[]{:S(2)}) collective-permute-start(f32[64,2048]{1,0:T(8,128)} %param.15), channel_id=1, source_target_pairs={{0,1},{1,0},{2,3},{3,2},{4,5},{5,4},{6,7},{7,6},{8,9},{9,8},{10,11... | collective-permute-start | bytes 1572872 | tf_op jit(solution)/shard_map/ppermute | solution.py:31
  123.8 1.1 copy_bitcast_fusion.1
  124.9 7.9 %all-to-all-done = f32[64,32,128]{2,1,0:T(8,128)S(1)} async-done(((f32[64,32,128]{2,1,0:T(8,128)}), f32[64,32,128]{2,1,0:T(8,128)S(1)}, u32[]{:S(2)}, u32[]{:S(2)}) %all-to-all-start) | async-done | bytes 1048608 | tf_op jit(solution)/shard_map/all_to_all | solution.py:324
  132.9 0.7 broadcast_in_dim.8
  133.7 3.5 %all-to-all-start.1 = ((f32[16,32,128]{2,1,0:T(8,128)}), f32[16,32,128]{2,1,0:T(8,128)S(1)}, u32[]{:S(2)}, u32[]{:S(2)}) async-start(f32[16,32,128]{2,1,0:T(8,128)} %broadcast_in_dim.8), calls=%async_computation.1 | async-start | bytes 524288 | tf_op jit(solution)/shard_map/all_to_all | solution.py:329
  137.3 7.4 %all-to-all-done.1 = f32[16,32,128]{2,1,0:T(8,128)S(1)} async-done(((f32[16,32,128]{2,1,0:T(8,128)}), f32[16,32,128]{2,1,0:T(8,128)S(1)}, u32[]{:S(2)}, u32[]{:S(2)}) %all-to-all-start.1) | async-done | bytes 262176 | tf_op jit(solution)/shard_map/all_to_all | solution.py:329
  144.7 1.1 convolution_bitcast_fusion
  145.9 1.1 broadcast_in_dim.18
  147.0 4.9 %all-to-all-start.2 = ((f32[64,32,128]{2,1,0:T(8,128)}), f32[64,32,128]{2,1,0:T(8,128)S(1)}, u32[]{:S(2)}, u32[]{:S(2)}) async-start(f32[64,32,128]{2,1,0:T(8,128)} %broadcast_in_dim.18), calls=%async_computation.2 | async-start | bytes 2097152 | tf_op jit(solution)/shard_map/all_to_all | solution.py:336
  151.9 1.9 copy-done.2
  153.8 3.8 %shard_map.98.up = bf16[3,512,2048]{2,1,0:T(8,128)(2,1)S(1)} custom-call(s32[3,16,1]{2,1,0:T(8,128)S(1)} %copy-done.6, s32[3,16,1]{2,1,0:T(8,128)S(1)} %copy-done.8, f32[3,128,2048]{2,1,0:T(8,128)S(1)} %bitcast.39, f32[3,128,2048]{2,1,0:T(8,128)} %collective-permute-done.21.part), custom_call_target="tpu_custom_call" | custom-call | tf_op jit(solution)/shard_map/pallas_call | solution.py:273
  157.6 2.7 %copy-done = bf16[3,512,2048]{2,1,0:T(8,128)(2,1)} copy-done((bf16[3,512,2048]{2,1,0:T(8,128)(2,1)}, bf16[3,512,2048]{2,1,0:T(8,128)(2,1)S(1)}, u32[]{:S(2)}) %copy-start) | copy-done | bytes 6291480
  160.3 5.4 %all-to-all-done.2 = f32[64,32,128]{2,1,0:T(8,128)S(1)} async-done(((f32[64,32,128]{2,1,0:T(8,128)}), f32[64,32,128]{2,1,0:T(8,128)S(1)}, u32[]{:S(2)}, u32[]{:S(2)}) %all-to-all-start.2) | async-done | bytes 1048608 | tf_op jit(solution)/shard_map/all_to_all | solution.py:336
  165.7 2.8 %copy-done.1 = bf16[3,512,2048]{2,1,0:T(8,128)(2,1)S(1)} copy-done((bf16[3,512,2048]{2,1,0:T(8,128)(2,1)S(1)}, bf16[3,512,2048]{2,1,0:T(8,128)(2,1)}, u32[]{:S(2)}) %copy-start.1) | copy-done | bytes 6291480
  168.5 2.4 %shard_map.99.refs_0_ = f32[3,256,128]{2,1,0:T(8,128)S(1)} custom-call(s32[3]{0:T(128)S(1)} %copy-done.9, f32[4,16,32,128]{3,2,1,0:T(8,128)S(1)} %bitcast.36, f32[3,256,128]{2,1,0:T(8,128)S(1)} %copy-done.4, bf16[3,512,2048]{2,1,0:T(8,128)(2,1)S(1)} %copy-done.1), custom_call_target="tpu_custom_call" | custom-call | tf_op jit(solution)/shard_map/pallas_call | solution.py:261
  171.0 1.4 collective-permute-start.23
  173.4 2.3 collective-permute-start.27
  175.7 1.9 collective-permute-done.22.refs_1_
  177.7 5.4 %collective-permute-done.23.refs_2_ = f32[3,256,128]{2,1,0:T(8,128)S(1)} collective-permute-done((f32[3,256,128]{2,1,0:T(8,128)S(1)}, f32[3,256,128]{2,1,0:T(8,128)S(1)}, u32[]{:S(2)}, u32[]{:S(2)}) %collective-permute-start.23) | collective-permute-done | bytes 393248 | tf_op jit(solution)/shard_map/ppermute | solution.py:27
  183.1 0.9 collective-permute-start.29
  184.6 2.1 collective-permute-start.31
  188.2 6.2 %collective-permute-done.29.refs_4_ = f32[3,256,128]{2,1,0:T(8,128)} collective-permute-done((f32[3,256,128]{2,1,0:T(8,128)S(1)}, f32[3,256,128]{2,1,0:T(8,128)}, u32[]{:S(2)}, u32[]{:S(2)}) %collective-permute-start.29) | collective-permute-done | bytes 393248 | tf_op jit(solution)/shard_map/ppermute | solution.py:27
  194.4 1.4 collective-permute-start.34
  195.8 1.9 collective-permute-done.30.refs_5_
  197.7 1.2 collective-permute-done.31.refs_6_
  199.1 3.6 %collective-permute-done.33.refs_8_ = f32[3,256,128]{2,1,0:T(8,128)} collective-permute-done((f32[3,256,128]{2,1,0:T(8,128)}, f32[3,256,128]{2,1,0:T(8,128)}, u32[]{:S(2)}, u32[]{:S(2)}) %collective-permute-start.33) | collective-permute-done | bytes 393248 | tf_op jit(solution)/shard_map/ppermute | solution.py:27
  202.8 2.2 collective-permute-start.37
  205.0 5.1 %shard_map.100.refs_0_ = f32[3,256,128]{2,1,0:T(8,128)} custom-call(s32[3]{0:T(128)} %pad_add_fusion.pos, f32[3,256,128]{2,1,0:T(8,128)} %copy-done.3, f32[3,256,128]{2,1,0:T(8,128)} %copy-done.20, f32[3,256,128]{2,1,0:T(8,128)} %copy-done.22, f32[3,256,128]{2,1,0:T(8,128)} %collective-permute-done.24.refs_3_, f32[3,128,4096]{2,1,0:T(8,128)} %bitcast.45, ...), custom_call_target="tpu_custom_call" | custom-call | tf_op jit(solution)/shard_map/pallas_call | solution.py:221
  210.1 7.8 %shard_map.101.total = f32[3,256,128]{2,1,0:T(8,128)} custom-call(s32[3]{0:T(128)} %pad_add_fusion.pos, f32[3,256,128]{2,1,0:T(8,128)} %shard_map.100.refs_0_, f32[3,256,128]{2,1,0:T(8,128)} %copy-done.23, f32[3,256,128]{2,1,0:T(8,128)} %collective-permute-done.27.refs_2_, f32[3,256,128]{2,1,0:T(8,128)} %copy-done.24, ...), custom_call_target="tpu_custom_call" | custom-call | tf_op jit(solution)/shard_map/pallas_call | solution.py:221
  218.0 5.4 %shard_map.102 = (f32[3,128,256]{2,1,0:T(8,128)}, f32[3,128,128]{2,1,0:T(8,128)}) custom-call(s32[3]{0:T(128)} %pad_add_fusion.pos, f32[3,256,128]{2,1,0:T(8,128)} %shard_map.101.total, f32[3,256,128]{2,1,0:T(8,128)} %collective-permute-done.34.refs_0_, f32[3,256,128]{2,1,0:T(8,128)} %collective-permute-done.35.refs_1_, ...), custom_call_target="tpu_custom_call" | custom-call | tf_op jit(solution)/shard_map/pallas_call | solution.py:250
  223.5 11.3 %collective-permute-start.38 = (f32[3,128,128]{2,1,0:T(8,128)}, f32[3,128,128]{2,1,0:T(8,128)S(1)}, u32[]{:S(2)}, u32[]{:S(2)}) collective-permute-start(f32[3,128,128]{2,1,0:T(8,128)} %get-tuple-element.27), channel_id=1, source_target_pairs={{0,1},{1,0},{2,3},{3,2},{4,5},{5,4},{6,7},{7,6},{8,9},{9,8},{10,11... | collective-permute-start | bytes 589832 | tf_op jit(solution)/shard_map/ppermute | solution.py:31
  235.0 1.2 collective-permute-done.39
  236.3 0.7 copy.36
  (102 shorter events, 7.9 us)
Async XLA Ops:
  1.7 2.5 %collective-permute-start = (f32[3,128,128]{2,1,0:T(8,128)S(1)}, f32[3,128,128]{2,1,0:T(8,128)S(1)}, u32[]{:S(2)}, u32[]{:S(2)}) collective-permute-start(f32[3,128,128]{2,1,0:T(8,128)S(1)} %get-tuple-element.33), channel_id=1, source_target_pairs={{0,1},{1,0},{2,3},{3,2},{4,5},{5,4},{6,7},{7,6},{8,9},{9,8},{10,11... | collective-permute-start | bytes 589832 | tf_op jit(solution)/shard_map/ppermute | solution.py:31
  4.3 80.4 %copy-start.10 = (f32[3,256,128]{2,1,0:T(8,128)}, f32[3,256,128]{2,1,0:T(8,128)S(1)}, u32[]{:S(2)}) copy-start(f32[3,256,128]{2,1,0:T(8,128)S(1)} %maximum_select_fusion.2.refs_0_) | copy-start | bytes 1179652
  4.3 76.9 %collective-permute-start.6 = (f32[3,128,4096]{2,1,0:T(8,128)}, f32[3,128,4096]{2,1,0:T(8,128)}, u32[]{:S(2)}, u32[]{:S(2)}) collective-permute-start(f32[3,128,4096]{2,1,0:T(8,128)} %bitcast.40), channel_id=1, source_target_pairs={{0,1},{1,0},{2,3},{3,2},{4,5},{5,4},{6,7},{7,6},{8,9},{9,8},{10,11... | collective-permute-start | bytes 18874376 | tf_op jit(solution)/shard_map/ppermute | solution.py:31
  4.7 7.6 %collective-permute-start.3 = (f32[3,256,128]{2,1,0:T(8,128)S(1)}, f32[3,256,128]{2,1,0:T(8,128)S(1)}, u32[]{:S(2)}, u32[]{:S(2)}) collective-permute-start(f32[3,256,128]{2,1,0:T(8,128)S(1)} %maximum_select_fusion.2.refs_0_), channel_id=1, source_target_pairs={{0,6},{1,25},{2,0},{3,27},{4,2},{5,29},{6,4},{7,31},{8,14},{9,1},{... | collective-permute-start | bytes 1179656 | tf_op jit(solution)/shard_map/ppermute | solution.py:27
  12.3 51.7 %copy-start.11 = (f32[3,256,128]{2,1,0:T(8,128)}, f32[3,256,128]{2,1,0:T(8,128)S(1)}, u32[]{:S(2)}) copy-start(f32[3,256,128]{2,1,0:T(8,128)S(1)} %collective-permute-done.3.refs_1_) | copy-start | bytes 1179652
  12.3 161.1 %collective-permute-start.25 = (f32[3,128,4096]{2,1,0:T(8,128)}, f32[3,128,4096]{2,1,0:T(8,128)}, u32[]{:S(2)}, u32[]{:S(2)}) collective-permute-start(f32[3,128,4096]{2,1,0:T(8,128)} %bitcast.44), channel_id=1, source_target_pairs={{0,1},{1,0},{2,3},{3,2},{4,5},{5,4},{6,7},{7,6},{8,9},{9,8},{10,11... | collective-permute-start | bytes 18874376 | tf_op jit(solution)/shard_map/ppermute | solution.py:31
  13.0 84.7 %collective-permute-start.19 = (f32[3,2048,128]{2,1,0:T(8,128)}, f32[3,2048,128]{2,1,0:T(8,128)}, u32[]{:S(2)}, u32[]{:S(2)}) collective-permute-start(f32[3,2048,128]{2,1,0:T(8,128)} %bitcast.48), channel_id=1, source_target_pairs={{0,1},{1,0},{2,3},{3,2},{4,5},{5,4},{6,7},{7,6},{8,9},{9,8},{10,11... | collective-permute-start | bytes 9437192 | tf_op jit(solution)/shard_map/ppermute | solution.py:31
  13.0 18.3 %collective-permute-start.4 = (f32[3,256,128]{2,1,0:T(8,128)S(1)}, f32[3,256,128]{2,1,0:T(8,128)S(1)}, u32[]{:S(2)}, u32[]{:S(2)}) collective-permute-start(f32[3,256,128]{2,1,0:T(8,128)S(1)} %maximum_select_fusion.2.refs_0_), channel_id=1, source_target_pairs={{0,2},{1,9},{2,4},{3,11},{4,6},{5,13},{6,0},{7,15},{8,10},{9,17},{... | collective-permute-start | bytes 1179656 | tf_op jit(solution)/shard_map/ppermute | solution.py:27
  15.1 74.7 %copy-start.5 = (s32[3,16,1]{2,1,0:T(8,128)}, s32[3,16,1]{2,1,0:T(8,128)S(1)}, u32[]{:S(2)}) copy-start(s32[3,16,1]{2,1,0:T(8,128)S(1)} %copy.30.mask_own) | copy-start | bytes 580
  15.1 13.2 %collective-permute-start.2 = (s32[3,16,1]{2,1,0:T(8,128)S(1)}, s32[3,16,1]{2,1,0:T(8,128)S(1)}, u32[]{:S(2)}, u32[]{:S(2)}) collective-permute-start(s32[3,16,1]{2,1,0:T(8,128)S(1)} %copy.30.mask_own), channel_id=1, source_target_pairs={{0,1},{1,0},{2,3},{3,2},{4,5},{5,4},{6,7},{7,6},{8,9},{9,8},{10,11... | collective-permute-start | bytes 584 | tf_op jit(solution)/shard_map/ppermute | solution.py:31
  28.4 61.5 %copy-start.7 = (s32[3,16,1]{2,1,0:T(8,128)}, s32[3,16,1]{2,1,0:T(8,128)S(1)}, u32[]{:S(2)}) copy-start(s32[3,16,1]{2,1,0:T(8,128)S(1)} %collective-permute-done.2.mask_part) | copy-start | bytes 580
  28.4 9.7 %collective-permute-start.5 = (f32[3,256,128]{2,1,0:T(8,128)S(1)}, f32[3,256,128]{2,1,0:T(8,128)S(1)}, u32[]{:S(2)}, u32[]{:S(2)}) collective-permute-start(f32[3,256,128]{2,1,0:T(8,128)S(1)} %maximum_select_fusion.2.refs_0_), channel_id=1, source_target_pairs={{0,4},{1,17},{2,6},{3,19},{4,0},{5,21},{6,2},{7,23},{8,12},{9,25},... | collective-permute-start | bytes 1179656 | tf_op jit(solution)/shard_map/ppermute | solution.py:27
  31.4 40.5 %copy-start.12 = (f32[3,256,128]{2,1,0:T(8,128)}, f32[3,256,128]{2,1,0:T(8,128)S(1)}, u32[]{:S(2)}) copy-start(f32[3,256,128]{2,1,0:T(8,128)S(1)} %collective-permute-done.4.refs_2_) | copy-start | bytes 1179652
  31.4 11.0 %collective-permute-start.7 = (f32[3,256,128]{2,1,0:T(8,128)S(1)}, f32[3,256,128]{2,1,0:T(8,128)S(1)}, u32[]{:S(2)}, u32[]{:S(2)}) collective-permute-start(f32[3,256,128]{2,1,0:T(8,128)S(1)} %maximum_select_fusion.2.refs_0_), channel_id=1, source_target_pairs={{0,8},{1,3},{2,10},{3,5},{4,12},{5,7},{6,14},{7,1},{8,16},{9,11},{... | collective-permute-start | bytes 1179656 | tf_op jit(solution)/shard_map/ppermute | solution.py:27
  38.1 33.9 %copy-start.13 = (f32[3,256,128]{2,1,0:T(8,128)}, f32[3,256,128]{2,1,0:T(8,128)S(1)}, u32[]{:S(2)}) copy-start(f32[3,256,128]{2,1,0:T(8,128)S(1)} %collective-permute-done.5.refs_3_) | copy-start | bytes 1179652
  38.1 9.1 %collective-permute-start.8 = (f32[3,256,128]{2,1,0:T(8,128)S(1)}, f32[3,256,128]{2,1,0:T(8,128)S(1)}, u32[]{:S(2)}, u32[]{:S(2)}) collective-permute-start(f32[3,256,128]{2,1,0:T(8,128)S(1)} %maximum_select_fusion.2.refs_0_), channel_id=1, source_target_pairs={{0,24},{1,7},{2,26},{3,1},{4,28},{5,3},{6,30},{7,5},{8,0},{9,15},{... | collective-permute-start | bytes 1179656 | tf_op jit(solution)/shard_map/ppermute | solution.py:27
  42.4 33.3 %copy-start.14 = (f32[3,256,128]{2,1,0:T(8,128)}, f32[3,256,128]{2,1,0:T(8,128)S(1)}, u32[]{:S(2)}) copy-start(f32[3,256,128]{2,1,0:T(8,128)S(1)} %collective-permute-done.7.refs_1_) | copy-start | bytes 1179652
  42.4 8.9 %collective-permute-start.10 = (f32[3,256,128]{2,1,0:T(8,128)S(1)}, f32[3,256,128]{2,1,0:T(8,128)S(1)}, u32[]{:S(2)}, u32[]{:S(2)}) collective-permute-start(f32[3,256,128]{2,1,0:T(8,128)S(1)} %collective-permute-done.3.refs_1_), channel_id=1, source_target_pairs={{0,24},{1,7},{2,26},{3,1},{4,28},{5,3},{6,30},{7,5},{8,0},{9,15},{... | collective-permute-start | bytes 1179656 | tf_op jit(solution)/shard_map/ppermute | solution.py:27
  47.2 33.9 %copy-start.15 = (f32[3,256,128]{2,1,0:T(8,128)}, f32[3,256,128]{2,1,0:T(8,128)S(1)}, u32[]{:S(2)}) copy-start(f32[3,256,128]{2,1,0:T(8,128)S(1)} %collective-permute-done.8.refs_2_) | copy-start | bytes 1179652
  47.2 8.7 %collective-permute-start.11 = (f32[3,256,128]{2,1,0:T(8,128)S(1)}, f32[3,256,128]{2,1,0:T(8,128)}, u32[]{:S(2)}, u32[]{:S(2)}) collective-permute-start(f32[3,256,128]{2,1,0:T(8,128)S(1)} %collective-permute-done.4.refs_2_), channel_id=1, source_target_pairs={{0,8},{1,3},{2,10},{3,5},{4,12},{5,7},{6,14},{7,1},{8,16},{9,11},{... | collective-permute-start | bytes 1179656 | tf_op jit(solution)/shard_map/ppermute | solution.py:27
  51.4 29.7 %copy-start.16 = (f32[3,256,128]{2,1,0:T(8,128)}, f32[3,256,128]{2,1,0:T(8,128)S(1)}, u32[]{:S(2)}) copy-start(f32[3,256,128]{2,1,0:T(8,128)S(1)} %collective-permute-done.10.refs_4_) | copy-start | bytes 1179652
  51.4 8.2 %collective-permute-start.12 = (f32[3,256,128]{2,1,0:T(8,128)S(1)}, f32[3,256,128]{2,1,0:T(8,128)S(1)}, u32[]{:S(2)}, u32[]{:S(2)}) collective-permute-start(f32[3,256,128]{2,1,0:T(8,128)S(1)} %collective-permute-done.4.refs_2_), channel_id=1, source_target_pairs={{0,24},{1,7},{2,26},{3,1},{4,28},{5,3},{6,30},{7,5},{8,0},{9,15},{... | collective-permute-start | bytes 1179656 | tf_op jit(solution)/shard_map/ppermute | solution.py:27
  55.8 8.1 %collective-permute-start.13 = (f32[3,256,128]{2,1,0:T(8,128)S(1)}, f32[3,256,128]{2,1,0:T(8,128)S(1)}, u32[]{:S(2)}, u32[]{:S(2)}) collective-permute-start(f32[3,256,128]{2,1,0:T(8,128)S(1)} %collective-permute-done.5.refs_3_), channel_id=1, source_target_pairs={{0,8},{1,3},{2,10},{3,5},{4,12},{5,7},{6,14},{7,1},{8,16},{9,11},{... | collective-permute-start | bytes 1179656 | tf_op jit(solution)/shard_map/ppermute | solution.py:27
  59.6 21.5 %copy-start.17 = (f32[3,256,128]{2,1,0:T(8,128)}, f32[3,256,128]{2,1,0:T(8,128)S(1)}, u32[]{:S(2)}) copy-start(f32[3,256,128]{2,1,0:T(8,128)S(1)} %collective-permute-done.12.refs_6_) | copy-start | bytes 1179652
  59.6 8.1 %collective-permute-start.14 = (f32[3,256,128]{2,1,0:T(8,128)S(1)}, f32[3,256,128]{2,1,0:T(8,128)}, u32[]{:S(2)}, u32[]{:S(2)}) collective-permute-start(f32[3,256,128]{2,1,0:T(8,128)S(1)} %collective-permute-done.5.refs_3_), channel_id=1, source_target_pairs={{0,24},{1,7},{2,26},{3,1},{4,28},{5,3},{6,30},{7,5},{8,0},{9,15},{... | collective-permute-start | bytes 1179656 | tf_op jit(solution)/shard_map/ppermute | solution.py:27
  64.0 17.2 %copy-start.18 = (f32[3,256,128]{2,1,0:T(8,128)}, f32[3,256,128]{2,1,0:T(8,128)S(1)}, u32[]{:S(2)}) copy-start(f32[3,256,128]{2,1,0:T(8,128)S(1)} %collective-permute-done.13.refs_7_) | copy-start | bytes 1179652
  64.0 7.9 %collective-permute-start.9 = (f32[3,256,128]{2,1,0:T(8,128)S(1)}, f32[3,256,128]{2,1,0:T(8,128)}, u32[]{:S(2)}, u32[]{:S(2)}) collective-permute-start(f32[3,256,128]{2,1,0:T(8,128)S(1)} %collective-permute-done.3.refs_1_), channel_id=1, source_target_pairs={{0,8},{1,3},{2,10},{3,5},{4,12},{5,7},{6,14},{7,1},{8,16},{9,11},{... | collective-permute-start | bytes 1179656 | tf_op jit(solution)/shard_map/ppermute | solution.py:27
  67.7 7.9 %collective-permute-start.15 = (f32[3,256,128]{2,1,0:T(8,128)S(1)}, f32[3,256,128]{2,1,0:T(8,128)S(1)}, u32[]{:S(2)}, u32[]{:S(2)}) collective-permute-start(f32[3,256,128]{2,1,0:T(8,128)S(1)} %collective-permute-done.8.refs_2_), channel_id=1, source_target_pairs={{0,24},{1,7},{2,26},{3,1},{4,28},{5,3},{6,30},{7,5},{8,0},{9,15},{... | collective-permute-start | bytes 1179656 | tf_op jit(solution)/shard_map/ppermute | solution.py:27
  71.9 9.1 %collective-permute-start.16 = (f32[3,256,128]{2,1,0:T(8,128)S(1)}, f32[3,256,128]{2,1,0:T(8,128)S(1)}, u32[]{:S(2)}, u32[]{:S(2)}) collective-permute-start(f32[3,256,128]{2,1,0:T(8,128)S(1)} %collective-permute-done.10.refs_4_), channel_id=1, source_target_pairs={{0,24},{1,7},{2,26},{3,1},{4,28},{5,3},{6,30},{7,5},{8,0},{9,15},{... | collective-permute-start | bytes 1179656 | tf_op jit(solution)/shard_map/ppermute | solution.py:27
  75.7 76.2 %collective-permute-start.21 = (f32[3,128,2048]{2,1,0:T(8,128)}, f32[3,128,2048]{2,1,0:T(8,128)}, u32[]{:S(2)}, u32[]{:S(2)}) collective-permute-start(f32[3,128,2048]{2,1,0:T(8,128)} %bitcast.38), channel_id=1, source_target_pairs={{0,1},{1,0},{2,3},{3,2},{4,5},{5,4},{6,7},{7,6},{8,9},{9,8},{10,11... | collective-permute-start | bytes 9437192 | tf_op jit(solution)/shard_map/ppermute | solution.py:31
  81.0 16.6 %collective-permute-start.17 = (f32[3,256,128]{2,1,0:T(8,128)}, f32[3,256,128]{2,1,0:T(8,128)}, u32[]{:S(2)}, u32[]{:S(2)}) collective-permute-start(f32[3,256,128]{2,1,0:T(8,128)} %collective-permute-done.11.refs_5_), channel_id=1, source_target_pairs={{0,8},{1,3},{2,10},{3,5},{4,12},{5,7},{6,14},{7,1},{8,16},{9,11},{... | collective-permute-start | bytes 1179656 | tf_op jit(solution)/shard_map/ppermute | solution.py:27
  81.8 15.9 %collective-permute-start.18 = (f32[3,256,128]{2,1,0:T(8,128)}, f32[3,256,128]{2,1,0:T(8,128)}, u32[]{:S(2)}, u32[]{:S(2)}) collective-permute-start(f32[3,256,128]{2,1,0:T(8,128)} %collective-permute-done.14.refs_8_), channel_id=1, source_target_pairs={{0,24},{1,7},{2,26},{3,1},{4,28},{5,3},{6,30},{7,5},{8,0},{9,15},{... | collective-permute-start | bytes 1179656 | tf_op jit(solution)/shard_map/ppermute | solution.py:27
  97.7 20.9 %copy-start.26 = (f32[64,256]{1,0:T(8,128)S(1)}, f32[64,256]{1,0:T(8,128)}, u32[]{:S(2)}) copy-start(f32[64,256]{1,0:T(8,128)} %param.9) | copy-start | bytes 196612
  108.4 43.5 %copy-start.6 = (s32[3,16,1]{2,1,0:T(8,128)S(1)}, s32[3,16,1]{2,1,0:T(8,128)}, u32[]{:S(2)}) copy-start(s32[3,16,1]{2,1,0:T(8,128)} %copy-done.5) | copy-start | bytes 580
  108.4 43.5 %copy-start.8 = (s32[3,16,1]{2,1,0:T(8,128)S(1)}, s32[3,16,1]{2,1,0:T(8,128)}, u32[]{:S(2)}) copy-start(s32[3,16,1]{2,1,0:T(8,128)} %copy-done.7) | copy-start | bytes 580
  108.5 24.3 %all-to-all-start = ((f32[64,32,128]{2,1,0:T(8,128)}), f32[64,32,128]{2,1,0:T(8,128)S(1)}, u32[]{:S(2)}, u32[]{:S(2)}) async-start(f32[64,32,128]{2,1,0:T(8,128)} %bitcast.50), calls=%async_computation | async-start | bytes 2097152 | tf_op jit(solution)/shard_map/all_to_all | solution.py:324
  118.7 18.5 %collective-permute-start.20 = (f32[64,2048]{1,0:T(8,128)}, f32[64,2048]{1,0:T(8,128)S(1)}, u32[]{:S(2)}, u32[]{:S(2)}) collective-permute-start(f32[64,2048]{1,0:T(8,128)} %param.15), channel_id=1, source_target_pairs={{0,1},{1,0},{2,3},{3,2},{4,5},{5,4},{6,7},{7,6},{8,9},{9,8},{10,11... | collective-permute-start | bytes 1572872 | tf_op jit(solution)/shard_map/ppermute | solution.py:31
  123.7 9.1 %collective-permute-start.1 = (f32[64,128]{0,1:T(8,128)S(1)}, f32[64,128]{0,1:T(8,128)S(1)}, u32[]{:S(2)}, u32[]{:S(2)}) collective-permute-start(f32[64,128]{0,1:T(8,128)S(1)} %get-tuple-element.35), channel_id=1, source_target_pairs={{0,1},{1,0},{2,3},{3,2},{4,5},{5,4},{6,7},{7,6},{8,9},{9,8},{10,11... | collective-permute-start | bytes 98312 | tf_op jit(solution)/shard_map/ppermute | solution.py:31
  133.7 11.0 %all-to-all-start.1 = ((f32[16,32,128]{2,1,0:T(8,128)}), f32[16,32,128]{2,1,0:T(8,128)S(1)}, u32[]{:S(2)}, u32[]{:S(2)}) async-start(f32[16,32,128]{2,1,0:T(8,128)} %broadcast_in_dim.8), calls=%async_computation.1 | async-start | bytes 524288 | tf_op jit(solution)/shard_map/all_to_all | solution.py:329
  147.0 18.7 %all-to-all-start.2 = ((f32[64,32,128]{2,1,0:T(8,128)}), f32[64,32,128]{2,1,0:T(8,128)S(1)}, u32[]{:S(2)}, u32[]{:S(2)}) async-start(f32[64,32,128]{2,1,0:T(8,128)} %broadcast_in_dim.18), calls=%async_computation.2 | async-start | bytes 2097152 | tf_op jit(solution)/shard_map/all_to_all | solution.py:336
  153.8 11.8 %copy-start.4 = (f32[3,256,128]{2,1,0:T(8,128)S(1)}, f32[3,256,128]{2,1,0:T(8,128)}, u32[]{:S(2)}) copy-start(f32[3,256,128]{2,1,0:T(8,128)} %get-tuple-element.23.interim) | copy-start | bytes 1179652
  153.8 11.9 %copy-start.9 = (s32[3]{0:T(128)S(1)}, s32[3]{0:T(128)}, u32[]{:S(2)}) copy-start(s32[3]{0:T(128)} %pad_add_fusion.pos) | copy-start | bytes 40
  170.9 34.1 %copy-start.3 = (f32[3,256,128]{2,1,0:T(8,128)}, f32[3,256,128]{2,1,0:T(8,128)S(1)}, u32[]{:S(2)}) copy-start(f32[3,256,128]{2,1,0:T(8,128)S(1)} %shard_map.99.refs_0_) | copy-start | bytes 1179652
  170.9 6.7 %collective-permute-start.22 = (f32[3,256,128]{2,1,0:T(8,128)S(1)}, f32[3,256,128]{2,1,0:T(8,128)S(1)}, u32[]{:S(2)}, u32[]{:S(2)}) collective-permute-start(f32[3,256,128]{2,1,0:T(8,128)S(1)} %shard_map.99.refs_0_), channel_id=1, source_target_pairs={{0,6},{1,25},{2,0},{3,27},{4,2},{5,29},{6,4},{7,31},{8,14},{9,1},{... | collective-permute-start | bytes 1179656 | tf_op jit(solution)/shard_map/ppermute | solution.py:27
  171.0 12.1 %collective-permute-start.23 = (f32[3,256,128]{2,1,0:T(8,128)S(1)}, f32[3,256,128]{2,1,0:T(8,128)S(1)}, u32[]{:S(2)}, u32[]{:S(2)}) collective-permute-start(f32[3,256,128]{2,1,0:T(8,128)S(1)} %shard_map.99.refs_0_), channel_id=1, source_target_pairs={{0,2},{1,9},{2,4},{3,11},{4,6},{5,13},{6,0},{7,15},{8,10},{9,17},{... | collective-permute-start | bytes 1179656 | tf_op jit(solution)/shard_map/ppermute | solution.py:27
  172.4 11.6 %collective-permute-start.24 = (f32[3,256,128]{2,1,0:T(8,128)S(1)}, f32[3,256,128]{2,1,0:T(8,128)}, u32[]{:S(2)}, u32[]{:S(2)}) collective-permute-start(f32[3,256,128]{2,1,0:T(8,128)S(1)} %shard_map.99.refs_0_), channel_id=1, source_target_pairs={{0,4},{1,17},{2,6},{3,19},{4,0},{5,21},{6,2},{7,23},{8,12},{9,25},... | collective-permute-start | bytes 1179656 | tf_op jit(solution)/shard_map/ppermute | solution.py:27
  173.0 11.6 %collective-permute-start.26 = (f32[3,256,128]{2,1,0:T(8,128)S(1)}, f32[3,256,128]{2,1,0:T(8,128)S(1)}, u32[]{:S(2)}, u32[]{:S(2)}) collective-permute-start(f32[3,256,128]{2,1,0:T(8,128)S(1)} %shard_map.99.refs_0_), channel_id=1, source_target_pairs={{0,8},{1,3},{2,10},{3,5},{4,12},{5,7},{6,14},{7,1},{8,16},{9,11},{... | collective-permute-start | bytes 1179656 | tf_op jit(solution)/shard_map/ppermute | solution.py:27
  173.4 13.3 %collective-permute-start.27 = (f32[3,256,128]{2,1,0:T(8,128)S(1)}, f32[3,256,128]{2,1,0:T(8,128)}, u32[]{:S(2)}, u32[]{:S(2)}) collective-permute-start(f32[3,256,128]{2,1,0:T(8,128)S(1)} %shard_map.99.refs_0_), channel_id=1, source_target_pairs={{0,24},{1,7},{2,26},{3,1},{4,28},{5,3},{6,30},{7,5},{8,0},{9,15},{... | collective-permute-start | bytes 1179656 | tf_op jit(solution)/shard_map/ppermute | solution.py:27
  177.6 27.4 %copy-start.20 = (f32[3,256,128]{2,1,0:T(8,128)}, f32[3,256,128]{2,1,0:T(8,128)S(1)}, u32[]{:S(2)}) copy-start(f32[3,256,128]{2,1,0:T(8,128)S(1)} %collective-permute-done.22.refs_1_) | copy-start | bytes 1179652
  177.6 9.9 %collective-permute-start.28 = (f32[3,256,128]{2,1,0:T(8,128)S(1)}, f32[3,256,128]{2,1,0:T(8,128)S(1)}, u32[]{:S(2)}, u32[]{:S(2)}) collective-permute-start(f32[3,256,128]{2,1,0:T(8,128)S(1)} %collective-permute-done.22.refs_1_), channel_id=1, source_target_pairs={{0,8},{1,3},{2,10},{3,5},{4,12},{5,7},{6,14},{7,1},{8,16},{9,11},{... | collective-permute-start | bytes 1179656 | tf_op jit(solution)/shard_map/ppermute | solution.py:27
  183.1 21.9 %copy-start.22 = (f32[3,256,128]{2,1,0:T(8,128)}, f32[3,256,128]{2,1,0:T(8,128)S(1)}, u32[]{:S(2)}) copy-start(f32[3,256,128]{2,1,0:T(8,128)S(1)} %collective-permute-done.23.refs_2_) | copy-start | bytes 1179652
  183.1 11.2 %collective-permute-start.29 = (f32[3,256,128]{2,1,0:T(8,128)S(1)}, f32[3,256,128]{2,1,0:T(8,128)}, u32[]{:S(2)}, u32[]{:S(2)}) collective-permute-start(f32[3,256,128]{2,1,0:T(8,128)S(1)} %collective-permute-done.22.refs_1_), channel_id=1, source_target_pairs={{0,24},{1,7},{2,26},{3,1},{4,28},{5,3},{6,30},{7,5},{8,0},{9,15},{... | collective-permute-start | bytes 1179656 | tf_op jit(solution)/shard_map/ppermute | solution.py:27
  184.0 13.7 %collective-permute-start.30 = (f32[3,256,128]{2,1,0:T(8,128)S(1)}, f32[3,256,128]{2,1,0:T(8,128)}, u32[]{:S(2)}, u32[]{:S(2)}) collective-permute-start(f32[3,256,128]{2,1,0:T(8,128)S(1)} %collective-permute-done.23.refs_2_), channel_id=1, source_target_pairs={{0,8},{1,3},{2,10},{3,5},{4,12},{5,7},{6,14},{7,1},{8,16},{9,11},{... | collective-permute-start | bytes 1179656 | tf_op jit(solution)/shard_map/ppermute | solution.py:27
  184.6 20.4 %copy-start.23 = (f32[3,256,128]{2,1,0:T(8,128)}, f32[3,256,128]{2,1,0:T(8,128)S(1)}, u32[]{:S(2)}) copy-start(f32[3,256,128]{2,1,0:T(8,128)S(1)} %collective-permute-done.26.refs_1_) | copy-start | bytes 1179652
  184.6 14.3 %collective-permute-start.31 = (f32[3,256,128]{2,1,0:T(8,128)S(1)}, f32[3,256,128]{2,1,0:T(8,128)S(1)}, u32[]{:S(2)}, u32[]{:S(2)}) collective-permute-start(f32[3,256,128]{2,1,0:T(8,128)S(1)} %collective-permute-done.23.refs_2_), channel_id=1, source_target_pairs={{0,24},{1,7},{2,26},{3,1},{4,28},{5,3},{6,30},{7,5},{8,0},{9,15},{... | collective-permute-start | bytes 1179656 | tf_op jit(solution)/shard_map/ppermute | solution.py:27
  186.7 16.1 %collective-permute-start.33 = (f32[3,256,128]{2,1,0:T(8,128)}, f32[3,256,128]{2,1,0:T(8,128)}, u32[]{:S(2)}, u32[]{:S(2)}) collective-permute-start(f32[3,256,128]{2,1,0:T(8,128)} %collective-permute-done.24.refs_3_), channel_id=1, source_target_pairs={{0,24},{1,7},{2,26},{3,1},{4,28},{5,3},{6,30},{7,5},{8,0},{9,15},{... | collective-permute-start | bytes 1179656 | tf_op jit(solution)/shard_map/ppermute | solution.py:27
  187.5 17.5 %copy-start.24 = (f32[3,256,128]{2,1,0:T(8,128)}, f32[3,256,128]{2,1,0:T(8,128)S(1)}, u32[]{:S(2)}) copy-start(f32[3,256,128]{2,1,0:T(8,128)S(1)} %collective-permute-done.28.refs_3_) | copy-start | bytes 1179652
  187.5 22.7 %collective-permute-start.32 = (f32[3,256,128]{2,1,0:T(8,128)}, f32[3,256,128]{2,1,0:T(8,128)}, u32[]{:S(2)}, u32[]{:S(2)}) collective-permute-start(f32[3,256,128]{2,1,0:T(8,128)} %collective-permute-done.24.refs_3_), channel_id=1, source_target_pairs={{0,8},{1,3},{2,10},{3,5},{4,12},{5,7},{6,14},{7,1},{8,16},{9,11},{... | collective-permute-start | bytes 1179656 | tf_op jit(solution)/shard_map/ppermute | solution.py:27
  194.4 23.6 %collective-permute-start.34 = (f32[3,256,128]{2,1,0:T(8,128)}, f32[3,256,128]{2,1,0:T(8,128)}, u32[]{:S(2)}, u32[]{:S(2)}) collective-permute-start(f32[3,256,128]{2,1,0:T(8,128)} %collective-permute-done.27.refs_2_), channel_id=1, source_target_pairs={{0,24},{1,7},{2,26},{3,1},{4,28},{5,3},{6,30},{7,5},{8,0},{9,15},{... | collective-permute-start | bytes 1179656 | tf_op jit(solution)/shard_map/ppermute | solution.py:27
  197.7 20.3 %collective-permute-start.35 = (f32[3,256,128]{2,1,0:T(8,128)}, f32[3,256,128]{2,1,0:T(8,128)}, u32[]{:S(2)}, u32[]{:S(2)}) collective-permute-start(f32[3,256,128]{2,1,0:T(8,128)} %collective-permute-done.29.refs_4_), channel_id=1, source_target_pairs={{0,24},{1,7},{2,26},{3,1},{4,28},{5,3},{6,30},{7,5},{8,0},{9,15},{... | collective-permute-start | bytes 1179656 | tf_op jit(solution)/shard_map/ppermute | solution.py:27
  198.9 19.1 %collective-permute-start.36 = (f32[3,256,128]{2,1,0:T(8,128)}, f32[3,256,128]{2,1,0:T(8,128)}, u32[]{:S(2)}, u32[]{:S(2)}) collective-permute-start(f32[3,256,128]{2,1,0:T(8,128)} %collective-permute-done.30.refs_5_), channel_id=1, source_target_pairs={{0,8},{1,3},{2,10},{3,5},{4,12},{5,7},{6,14},{7,1},{8,16},{9,11},{... | collective-permute-start | bytes 1179656 | tf_op jit(solution)/shard_map/ppermute | solution.py:27
  202.8 15.2 %collective-permute-start.37 = (f32[3,256,128]{2,1,0:T(8,128)}, f32[3,256,128]{2,1,0:T(8,128)}, u32[]{:S(2)}, u32[]{:S(2)}) collective-permute-start(f32[3,256,128]{2,1,0:T(8,128)} %collective-permute-done.33.refs_8_), channel_id=1, source_target_pairs={{0,24},{1,7},{2,26},{3,1},{4,28},{5,3},{6,30},{7,5},{8,0},{9,15},{... | collective-permute-start | bytes 1179656 | tf_op jit(solution)/shard_map/ppermute | solution.py:27
  223.5 13.5 %collective-permute-start.38 = (f32[3,128,128]{2,1,0:T(8,128)}, f32[3,128,128]{2,1,0:T(8,128)S(1)}, u32[]{:S(2)}, u32[]{:S(2)}) collective-permute-start(f32[3,128,128]{2,1,0:T(8,128)} %get-tuple-element.27), channel_id=1, source_target_pairs={{0,1},{1,0},{2,3},{3,2},{4,5},{5,4},{6,7},{7,6},{8,9},{9,8},{10,11... | collective-permute-start | bytes 589832 | tf_op jit(solution)/shard_map/ppermute | solution.py:31
  234.9 1.3 collective-permute-start.39
  (6 other events, 19.7 us)
